TPU v7x, 128 devices: a whole 4x4x4 slice. The times are simulated.
128 devices in a mesh: sub: 32 (over x, y_hi, z), lib: 4 (over y_lo, core).
Axes of the slice: x: 4, y: 4 (y_hi: 2, y_lo: 2; y = y_hi * 2 + y_lo), z: 4, core: 2. Of those that a mesh axis runs over, the one named last changes fastest.
Arguments:
- snap_start: bfloat16 [4, 256, 128, 256], P(None, 'sub'), may hold values from -20 to 20
- snap_end: bfloat16 [4, 256, 128, 256], P(None, 'sub'), may hold values from -20 to 20
- exponents: int32 [512, 7], P('lib'), may hold values from 0 to 2, as said below
Outputs:
- coefficients: float32 [4, 512], P(None, 'lib')
- fitted: float32 [4, 16384], P(None, ('sub', 'lib'))
Inputs may be any that keep to these rules, and one draw needn't show every extreme that they name: Each row holds four field exponents of 0 to 2 with total degree 1 to 3, then three derivative orders of 0 to 2; rows are distinct, each of the 30 such monomials appears in one row whose derivative orders are all zero, and each of the four fields to the first power alone appears with derivative orders (0, 0, 1) and with (0, 1, 1).
All inputs are finite; a program needn't handle non-finite values.
Results may differ from a plain program's by a relative error of at most 0.0024.
Values may be sent and summed in bfloat16 or wider, within the bound.
A program may use at most 64 MiB of HBM per device.

v0:
```python
import jax
import jax.numpy as jnp
from jax import lax
from jax.sharding import PartitionSpec as P

STRIDE = 8
RADIUS = 8
POWER = 6
ITERS = 10


highest = lax.Precision.HIGHEST
ridge_term = 0.1
shrink = 0.05
epsilon = 1e-06


def shifted(value, axis, steps):
    count = lax.axis_size(axis)
    first, last = (max(0, -steps), min(count, count - steps))
    return lax.ppermute(value, axis, [(source, source + steps) for source in range(first, last)])


def tap_table(length, centers_count, offset):
    cell_pos = jnp.arange(length, dtype=jnp.float32)
    centers = STRIDE * jnp.arange(centers_count, dtype=jnp.float32) + offset
    scaled = (cell_pos[:, None] - centers[None, :]) / RADIUS
    inside = jnp.abs(scaled) <= 1.0
    bump_base = 1.0 - scaled * scaled
    zeroth = bump_base * bump_base * bump_base
    first_order = 6.0 * scaled * bump_base * bump_base
    second = -6.0 * bump_base * (1.0 - 5.0 * scaled * scaled)
    stacked = jnp.stack([zeroth, first_order, second])
    return jnp.where(inside[None], stacked, jnp.zeros_like(stacked))


def select_taps(tap_stack, orders):
    pick_rows = (orders[:, None] == jnp.arange(3, dtype=jnp.int32)[None, :]).astype(jnp.float32)
    return jnp.einsum("tj,jlc->tlc", pick_rows, tap_stack, precision=highest)


def monomial_block(fields, powers):
    result = None
    for channel in range(4):
        values = fields[channel].astype(jnp.float32)[None]
        power_here = powers[:, channel][:, None, None, None]
        factor = jnp.where(
            power_here == 0,
            jnp.ones_like(values),
            jnp.where(power_here == 1, values, values * values),
        )
        result = factor if channel == 0 else result * factor
    return result.astype(jnp.bfloat16)


def weak_block(theta_block, x_table, y_table, z_table, orders):
    z_taps = select_taps(z_table, orders[:, 2]).astype(jnp.bfloat16)
    reduced = jnp.einsum("txyz,tzc->txyc", theta_block, z_taps, preferred_element_type=jnp.float32)
    reduced = jnp.einsum(
        "txyc,tyb->txbc", reduced, select_taps(y_table, orders[:, 1]), precision=highest
    )
    return jnp.einsum(
        "txbc,txa->tabc", reduced, select_taps(x_table, orders[:, 0]), precision=highest
    )


def local(snap_start, snap_end, exponents):
    term_count = exponents.shape[0]
    cells_x = snap_start.shape[1]
    height = snap_start.shape[2]
    width_z = snap_start.shape[3]
    x_count = cells_x // STRIDE
    plane_rows = height // STRIDE * (width_z // STRIDE)
    y_table = tap_table(height, height // STRIDE, 0)
    z_table = tap_table(width_z, width_z // STRIDE, 0)
    rim_width = RADIUS - 1
    rim_pair = shifted(
        (snap_start[:, cells_x - rim_width :], snap_end[:, cells_x - rim_width :]), "sub", 1
    )
    first_field = jnp.concatenate([rim_pair[0], snap_start], axis=1)
    last_field = jnp.concatenate([rim_pair[1], snap_end], axis=1)
    x_table = tap_table(cells_x + rim_width, x_count, rim_width)

    def term_block(block_rows):
        theta_block = monomial_block(first_field, block_rows[:, :4])
        return weak_block(theta_block, x_table, y_table, z_table, block_rows[:, 4:])

    library = lax.map(term_block, exponents.reshape(term_count // 8, 8, 7))
    library = library.reshape(term_count, -1, plane_rows)
    change = (last_field.astype(jnp.float32) - first_field.astype(jnp.float32)).astype(jnp.bfloat16)
    targets = weak_block(change, x_table, y_table, z_table, jnp.zeros((4, 3), jnp.int32)).reshape(
        4, -1, plane_rows
    )
    library = library.reshape(term_count, -1)
    targets = targets.reshape(4, -1)
    row_count = library.shape[1]
    lib_count = lax.axis_size("lib")
    sub_count = lax.axis_size("sub")
    lib_index = lax.axis_index("lib")
    total_terms = term_count * lib_count
    total_rows = row_count * sub_count
    shard_piece = lax.all_gather(library.astype(jnp.bfloat16), "lib", axis=0, tiled=True).astype(
        jnp.float32
    )
    squares = jnp.zeros((total_terms,), jnp.float32)
    gram_block = lax.dot_general(
        library,
        shard_piece,
        (((1,), (1,)), ((), ())),
        precision=highest,
        preferred_element_type=jnp.float32,
    )
    gram_rows = gram_block
    squares = lax.dynamic_update_slice_in_dim(
        squares, jnp.sum(shard_piece * shard_piece, axis=1), jnp.int32(0), 0
    )
    gram_rows, squares = (gram_rows, squares)
    cross_terms = lax.dot_general(
        library,
        targets,
        (((1,), (1,)), ((), ())),
        precision=highest,
        preferred_element_type=jnp.float32,
    )
    target_squares = jnp.sum(targets * targets, axis=1)
    gram_rows, squares, cross_terms, target_squares = lax.psum(
        (gram_rows, squares, cross_terms, target_squares), "sub"
    )
    row_offset = lib_index * term_count

    def collect_coef(part_coef):
        return lax.all_gather(part_coef, "lib", axis=1, tiled=True)

    column_scale = jnp.sqrt(squares / total_rows + epsilon)
    target_scale = jnp.sqrt(target_squares / total_rows + epsilon)
    own_scale = lax.dynamic_slice_in_dim(column_scale, row_offset, term_count)
    own_ids = row_offset + jnp.arange(term_count, dtype=jnp.int32)
    identity_part = (own_ids[:, None] == jnp.arange(total_terms, dtype=jnp.int32)[None, :]).astype(
        jnp.float32
    )
    normal_rows = (
        gram_rows / (total_rows * own_scale[:, None] * column_scale[None, :])
        + ridge_term * identity_part
    )
    normal_cross = cross_terms / (total_rows * own_scale[:, None] * target_scale[None, :])
    vector = jnp.full((total_terms,), total_terms ** (-0.5), jnp.float32)
    magnitude = jnp.ones((), jnp.float32)
    for sweep_index in range(POWER):
        applied = lax.all_gather(
            jnp.dot(normal_rows, vector, precision=highest), "lib", axis=0, tiled=True
        )
        magnitude = jnp.sqrt(jnp.sum(applied * applied))
        vector = applied / magnitude
    step_size = 1.0 / magnitude

    def descend(sweep_index, coeffs):
        own_coef = lax.dynamic_slice_in_dim(coeffs, row_offset, term_count, 1)
        gradient = (
            lax.dot_general(
                coeffs,
                normal_rows,
                (((1,), (1,)), ((), ())),
                precision=highest,
                preferred_element_type=jnp.float32,
            )
            - normal_cross.T
        )
        moved_coef = own_coef - step_size * gradient
        shrunk = jnp.sign(moved_coef) * jnp.maximum(jnp.abs(moved_coef) - step_size * shrink, 0.0)
        return collect_coef(shrunk)

    coeffs = lax.fori_loop(0, ITERS, descend, jnp.zeros((4, total_terms), jnp.float32))
    lib_coef = lax.dynamic_slice_in_dim(coeffs, lib_index * term_count, term_count, 1)
    lib_scale = lax.dynamic_slice_in_dim(column_scale, lib_index * term_count, term_count)
    fit_terms = jnp.dot(
        lib_coef / lib_scale[None, :],
        library,
        precision=highest,
        preferred_element_type=jnp.float32,
    )
    fitted = lax.psum_scatter(fit_terms, "lib", scatter_dimension=1, tiled=True)
    return (lib_coef, fitted)


def solution(mesh):
    placed = (P(None, "sub", None, None), P(None, "sub", None, None), P("lib", None))
    return jax.shard_map(
        local,
        mesh=mesh,
        in_specs=placed,
        out_specs=(P(None, "lib"), P(None, ("sub", "lib"))),
        check_vma=False,
    )
```

profile of v0, /device:TPU:1, one launch (start us, length us, event | category | flops | bytes accessed | tf_op | source)
XLA Modules:
  0.0 1000.0 jit_solution(18005302535938893821)
XLA Ops:
  22.3 31.5 %collective-permute-done = bf16[4,7,128,256]{3,2,1,0:T(8,128)(2,1)} collective-permute-done((bf16[4,7,128,256]{3,2,1,0:T(8,128)(2,1)}, bf16[4,7,128,256]{3,2,1,0:T(8,128)(2,1)}, u32[]{:S(2)}, u32[]{:S(2)}) %collective-permute-start) | collective-permute-done | bytes 1835040 | tf_op jit(solution)/shard_map/ppermute | solution.py:21
  55.7 37.4 %collective-permute-done.1 = bf16[4,7,128,256]{3,2,1,0:T(8,128)(2,1)} collective-permute-done((bf16[4,7,128,256]{3,2,1,0:T(8,128)(2,1)}, bf16[4,7,128,256]{3,2,1,0:T(8,128)(2,1)}, u32[]{:S(2)}, u32[]{:S(2)}) %collective-permute-start.1) | collective-permute-done | bytes 1835040 | tf_op jit(solution)/shard_map/ppermute | solution.py:21
  100.4 323.9 %while.22 = (s32[]{:T(128)}, f32[16,8,1,16,32]{4,3,2,1,0:T(8,128)S(1)}, s32[16,8,7]{2,1,0:T(8,128)S(1)}, f32[3,15,1]{1,0,2:T(4,128)S(1)}, f32[3,128,16]{1,0,2:T(...) while((s32[]{:T(128)}, f32[16,8,1,16,32]{4,3,2,1,0:T(8,128)S(1)}, ...), condition=%wide.region_1.2_spmd, body=%wide.region_0.1_spmd.sunk | while | flops 402870656 | bytes 60139724 | solution.py:88
  112.2 7.4 convolution_bitcast_fusion.14
  126.0 6.2 fusion.120
  132.4 7.4 convolution_bitcast_fusion.14
  146.2 6.2 fusion.120
  152.6 7.4 convolution_bitcast_fusion.14
  166.4 6.2 fusion.120
  172.8 7.4 convolution_bitcast_fusion.14
  186.6 6.2 fusion.120
  193.1 7.4 convolution_bitcast_fusion.14
  206.8 6.2 fusion.120
  213.3 7.4 convolution_bitcast_fusion.14
  227.1 6.2 fusion.120
  233.5 7.4 convolution_bitcast_fusion.14
  253.7 7.4 convolution_bitcast_fusion.14
  273.9 7.4 convolution_bitcast_fusion.14
  294.2 7.4 convolution_bitcast_fusion.14
  314.4 7.4 convolution_bitcast_fusion.14
  334.6 7.4 convolution_bitcast_fusion.14
  354.8 7.4 convolution_bitcast_fusion.14
  375.0 7.4 convolution_bitcast_fusion.14
  388.8 6.2 fusion.120
  395.3 7.4 convolution_bitcast_fusion.14
  415.5 7.4 convolution_bitcast_fusion.14
  424.7 8.6 all_gather.26
  435.1 85.1 %all-reduce = (f32[512]{0:T(512)S(1)}, f32[128,4]{0,1:T(4,128)S(1)}, f32[4]{0:T(128)S(1)}) all-reduce(f32[512]{0:T(512)S(1)} %multiply_reduce_fusion, f32[128,4]{0,1:T(4,128)S(1)} %fusion.70, f32[4]{0:T(128)S(1)} %multiply_reduce_fusion.1), channel_id=1, replica_groups=mesh['sub'=32,'lib'=4] {'sub'}, use_global_device_ids=true, to_apply=%region_4.5 | all-reduce | flops 1028 | bytes 8224 | tf_op jit(solution)/shard_map/psum | solution.py:126
  520.6 333.6 %all-reduce.3.cloned.1.call-done = f32[128,512]{1,0:T(8,128)} async-done(((f32[128,512]{1,0:T(8,128)}), f32[128,512]{1,0:T(8,128)}) %all-reduce.3.cloned.1.call-update) | async-done | bytes 262160 | tf_op jit(solution)/shard_map/psum | solution.py:126
  855.6 27.1 %all-gather = f32[4,1,128]{2,1,0:T(1,128)S(1)} all-gather(f32[1,1,128]{2,1,0:T(1,128)S(1)} %convolution_bitcast_fusion.10), channel_id=1, replica_groups=mesh['sub'=32,'lib'=4] {'lib'}, dimensions={0}, use_global_device_ids=true | all-gather | bytes 2560 | tf_op jit(solution)/shard_map/all_gather | solution.py:149
  917.8 54.8 %while.23 = (s32[]{:T(128)}, f32[4,512]{1,0:T(4,128)S(1)}, s32[]{:T(128)}, f32[]{:T(128)}, f32[128,512]{1,0:T(8,128)S(1)}, /*index=5*/f32[128,4]{0,1:T(4,128)S(1)}, f32[]{:T(128)}, s32[]{:T(128)}) while((s32[]{:T(128)}, f32[4,512]{1,0:T(4,128)S(1)}, s32[]{:T(128)}, f32[]{:T(128)}, f32[128,512]{1,0:T(8,128)S(1)}, ...), condition=%wide.region_15.16_spmd, body=%wide.region_14.15_spmd.sunk | while | flops 3149826 | bytes 286817 | solution.py:172
  974.0 17.7 %reduce-scatter.4.cloned.1.call-done = f32[128,4]{1,0:T(8,128)} async-done(((f32[512,4]{1,0:T(8,128)}), f32[128,4]{1,0:T(8,128)}) %reduce-scatter.4.cloned.1.call-update) | async-done | bytes 2064
  (303 shorter events, 276.5 us)
Async XLA Ops:
  7.2 8.9 copy-start.3
  7.2 847.0 %all-reduce.3.cloned.1.call-start = ((), (), s32[]{:S(2)}) async-start(), calls=%async_computation.1 | async-start | bytes 524288 | tf_op jit(solution)/shard_map/psum | solution.py:126
  10.3 11.3 %copy-start.6 = (s32[128,7]{0,1:T(8,128)S(1)}, s32[128,7]{0,1:T(8,128)}, u32[]{:S(2)}) copy-start(s32[128,7]{0,1:T(8,128)} %param.9) | copy-start | bytes 10756
  10.3 43.5 %collective-permute-start = (bf16[4,7,128,256]{3,2,1,0:T(8,128)(2,1)}, bf16[4,7,128,256]{3,2,1,0:T(8,128)(2,1)}, u32[]{:S(2)}, u32[]{:S(2)}) collective-permute-start(bf16[4,7,128,256]{3,2,1,0:T(8,128)(2,1)} %slice.48), channel_id=1, source_target_pairs={{0,4},{4,8},{8,12},{12,16},{16,20},{20,24},{24,28},{28,32},{32,36}... | collective-permute-start | bytes 5505032 | tf_op jit(solution)/shard_map/ppermute | solution.py:21
  17.4 75.7 %collective-permute-start.1 = (bf16[4,7,128,256]{3,2,1,0:T(8,128)(2,1)}, bf16[4,7,128,256]{3,2,1,0:T(8,128)(2,1)}, u32[]{:S(2)}, u32[]{:S(2)}) collective-permute-start(bf16[4,7,128,256]{3,2,1,0:T(8,128)(2,1)} %slice.49), channel_id=1, source_target_pairs={{0,4},{4,8},{8,12},{12,16},{16,20},{20,24},{24,28},{28,32},{32,36}... | collective-permute-start | bytes 5505032 | tf_op jit(solution)/shard_map/ppermute | solution.py:21
  21.5 34.0 %copy-start.2 = (bf16[4,8,128,256]{3,2,1,0:T(8,128)(2,1)S(1)}, bf16[4,8,128,256]{3,2,1,0:T(8,128)(2,1)}, u32[]{:S(2)}) copy-start(bf16[4,8,128,256]{3,2,1,0:T(8,128)(2,1)} %param.7) | copy-start | bytes 6291460
  55.4 37.7 %copy-start.4 = (bf16[4,8,128,256]{3,2,1,0:T(8,128)(2,1)S(1)}, bf16[4,8,128,256]{3,2,1,0:T(8,128)(2,1)}, u32[]{:S(2)}) copy-start(bf16[4,8,128,256]{3,2,1,0:T(8,128)(2,1)} %param.8) | copy-start | bytes 6291460
  55.7 40.2 %copy-start = (bf16[4,15,128,256]{3,2,1,0:T(8,128)(2,1)}, bf16[4,15,128,256]{3,2,1,0:T(8,128)(2,1)S(1)}, u32[]{:S(2)}) copy-start(bf16[4,15,128,256]{3,2,1,0:T(8,128)(2,1)S(1)} %constant_dynamic-update-slice_fusion.1) | copy-start | bytes 11796484
  101.4 3.3 copy-start.1
  121.6 3.3 copy-start.1
  141.8 3.3 copy-start.1
  162.0 3.3 copy-start.1
  182.2 3.3 copy-start.1
  202.5 3.3 copy-start.1
  222.7 3.3 copy-start.1
  242.9 3.3 copy-start.1
  263.1 3.3 copy-start.1
  283.3 3.3 copy-start.1
  303.5 3.3 copy-start.1
  323.8 3.3 copy-start.1
  344.0 3.3 copy-start.1
  364.2 3.3 copy-start.1
  384.4 3.3 copy-start.1
  404.6 3.3 copy-start.1
  520.4 471.3 %reduce-scatter.4.cloned.1.call-start = ((), (), s32[]{:S(2)}) async-start(), calls=%async_computation.2 | async-start | bytes 327680
  972.7 20.5 %copy-start.5 = (f32[4,128]{1,0:T(4,128)}, f32[4,128]{1,0:T(4,128)S(1)}, u32[]{:S(2)}) copy-start(f32[4,128]{1,0:T(4,128)S(1)} %constant_dynamic-slice_fusion) | copy-start | bytes 6148
Sparse Core Ops, SparseCore 0:
  520.5 333.6 all-reduce.2
  974.1 17.5 reduce-scatter.3
where the time goes:
time: 1000 us
  waiting for transfers between devices  420 us (42%)
  matrix products  259 us (26%)
  blocking collectives  198 us (20%)
  other arithmetic  79.8 us (8%)
  between operations  18.6 us (2%)
  local copies, waits for them, and re-layouts  12.4 us (1%)
    psum x1, waiting for transfers between devices, local(): lax.psum((gram_rows, squares, cross_terms, target_squares), 'sub')  334 us
    dot_general x17, matrix products, weak_block(): jnp.einsum('txyc,tyb->txbc', reduced, select_taps(y_table, orders[:, 1]),...  122 us
    dot_general x17, matrix products, weak_block(): jnp.einsum('txyz,tzc->txyc', theta_block, z_taps, preferred_element_type=...  102 us
    psum x1, blocking collectives, local(): lax.psum((gram_rows, squares, cross_terms, target_squares), 'sub')  85.1 us
    broadcast_in_dim x32, other arithmetic, monomial_block(): jnp.where(power_here == 1, values, values * values)  69.6 us
    ppermute x2, waiting for transfers between devices, shifted(): lax.ppermute(value, axis, [(source, source + steps) for source in range(f...  68.9 us
    all_gather x6, blocking collectives, local(): lax.all_gather(jnp.dot(normal_rows, vector, precision=highest), 'lib', ax...  52.5 us
    all_gather x10, blocking collectives, collect_coef(): return lax.all_gather(part_coef, 'lib', axis=1, tiled=True)  52.1 us
  transfers between devices with their start and end apart: 4, of which 4 were waited for; matrix products, arithmetic and copies ran while one was open for 0% of the time, Pallas kernels for 0%

commit v1 on v0

v1 whole, which is shorter than its diff:
```python
import functools

import jax
import jax.numpy as jnp
import ml_dtypes
import numpy as np
from jax import lax
from jax.experimental import pallas as pl
from jax.experimental.pallas import tpu as pltpu
from jax.sharding import PartitionSpec as P

STRIDE = 8
RADIUS = 8
POWER = 6
ITERS = 10
TERMS = 512
ROWS = 16384
RIDGE = 0.1
SHRINK = 0.05
EPSILON = 1e-06

CELLS_X = 8
CELLS_Y = 40
CELLS_XY = CELLS_X * CELLS_Y
WIDTH_Z = 256
CENTERS_Y = 4
CENTERS_Z = 32
TESTS = CENTERS_Y * CENTERS_Z

POWERS = [
    (a, b, c, e)
    for a in range(3)
    for b in range(3)
    for c in range(3)
    for e in range(3)
    if 1 <= a + b + c + e <= 3
]
PRODUCTS = len(POWERS) + 4
PAD = 16
TABLE = PRODUCTS * PAD
KEYS = 3 * TABLE
PICKED = TERMS + 16
TARGET_CODE = 4000

CHUNK = 16
BLOCKS = (
    ((0, 0), (0, 1), (0, 2), (0, 3), (3, 3)),
    ((1, 1), (1, 2), (1, 3), (2, 2), (2, 3)),
)
CHUNKS = 8 * len(BLOCKS[0]) + 1
CHIPS = 64
SPREAD = 25
UNSPREAD = 41

MESH = pl.DeviceIdType.MESH
f32 = jnp.float32
bf16 = jnp.bfloat16


def tap(order, offset):
    s = np.asarray(offset, np.float64) / RADIUS
    base = 1.0 - s * s
    value = (base**3, 6.0 * s * base**2, -6.0 * base * (1.0 - 5.0 * s * s))[order]
    return np.where(np.abs(s) <= 1.0, value, 0.0)


def split_pieces(values):
    high = values.astype(ml_dtypes.bfloat16)
    low = (values - high.astype(np.float64)).astype(ml_dtypes.bfloat16)
    return high, low


def plane_weights():
    x = np.arange(CELLS_X)[:, None]
    y = np.arange(CELLS_Y)[None, :]
    both = []
    for shift in (0, STRIDE):
        full = np.zeros((2, CENTERS_Y, PAD, CELLS_X, CELLS_Y))
        for side in range(2):
            for center in range(CENTERS_Y):
                for order_x in range(3):
                    for order_y in range(3):
                        full[side, center, order_x * 3 + order_y] = tap(
                            order_x, x - STRIDE * side
                        ) * tap(order_y, y - STRIDE * center - shift)
        high, low = split_pieces(full.reshape(2 * CENTERS_Y * PAD, CELLS_XY))
        both.append(np.concatenate([high, low]))
    return np.stack(both)


def depth_weights():
    z = np.arange(WIDTH_Z)[:, None]
    centers = STRIDE * np.arange(CENTERS_Z)[None, :]
    full = np.zeros((CENTERS_Y, WIDTH_Z, 3, CENTERS_Y, CENTERS_Z))
    for order in range(3):
        for center in range(CENTERS_Y):
            full[center, :, order, center, :] = tap(order, z - centers)
    return full.reshape(CENTERS_Y * WIDTH_Z, 3 * TESTS).astype(ml_dtypes.bfloat16)


def column_codes():
    codes = np.full((3, PRODUCTS, PAD), -2.0, np.float32)
    for index, (a, b, c, e) in enumerate(POWERS):
        for order_z in range(3):
            for plane in range(9):
                codes[order_z, index, plane] = (
                    (((a * 3 + b) * 3 + c) * 3 + e) * 27 + plane * 3 + order_z
                )
    for field in range(4):
        codes[0, len(POWERS) + field, 0] = TARGET_CODE + field
    return codes.reshape(1, KEYS)


def code_weights():
    return np.array([[729, 243, 81, 27, 9, 3, 1]], np.float32)


def position():
    sub = lax.axis_index("sub")
    lib = lax.axis_index("lib")
    return sub // 8, (sub // 4) % 2 * 2 + lib // 2, sub % 4, lib % 2


def chip_device(chip, core):
    y = chip // 4 % 4
    return {"sub": (chip // 16 * 2 + y // 2) * 4 + chip % 4, "lib": y % 2 * 2 + core}


def products(fields_ref, later_ref, wide_ref, theta_ref):
    for field in range(4):
        for x in range(CELLS_X):
            wide_ref[field, x * CELLS_Y : (x + 1) * CELLS_Y, :] = fields_ref[field, x].astype(f32)
            wide_ref[4 + field, x * CELLS_Y : (x + 1) * CELLS_Y, :] = later_ref[field, x].astype(
                f32
            )

    def rows(step, carry):
        at = pl.multiple_of(step * 16, 16)
        value = [wide_ref[field, pl.ds(at, 16), :] for field in range(4)]
        square = [v * v for v in value]
        pairs = {}
        for index, powers in enumerate(POWERS):
            result = None
            key = ()
            for field, power in enumerate(powers):
                if power == 0:
                    continue
                factor = value[field] if power == 1 else square[field]
                key = key + ((field, power),)
                if result is None:
                    result = factor
                elif key in pairs:
                    result = pairs[key]
                else:
                    result = result * factor
                    pairs[key] = result
            theta_ref[index, pl.ds(at, 16), :] = result.astype(bf16)
        for field in range(4):
            change = wide_ref[4 + field, pl.ds(at, 16), :] - value[field]
            theta_ref[len(POWERS) + field, pl.ds(at, 16), :] = change.astype(bf16)
        return carry

    lax.fori_loop(0, CELLS_XY // 16, rows, 0)


def plane_sums(weights_ref, theta_ref, plane_ref):
    half = 2 * CENTERS_Y * PAD

    def one(index, carry):
        both = jnp.dot(weights_ref[...], theta_ref[index], preferred_element_type=f32)
        total = both[:half] + both[half:]
        high = total.astype(bf16)
        low = (total - high.astype(f32)).astype(bf16)
        at = pl.multiple_of(index * PAD, PAD)
        for side in range(2):
            for center in range(CENTERS_Y):
                row = (side * CENTERS_Y + center) * PAD
                lanes = slice(center * WIDTH_Z, (center + 1) * WIDTH_Z)
                plane_ref[side, 0, pl.ds(at, PAD), lanes] = high[row : row + PAD]
                plane_ref[side, 1, pl.ds(at, PAD), lanes] = low[row : row + PAD]
        return carry

    lax.fori_loop(0, PRODUCTS, one, 0)


def depth_sums(plane_ref, depth_ref, table_ref, side):
    size = 2 * PAD * 17 // 2
    for start in range(0, TABLE, size):
        high = jnp.dot(
            plane_ref[side, 0, start : start + size], depth_ref[...], preferred_element_type=f32
        )
        low = jnp.dot(
            plane_ref[side, 1, start : start + size], depth_ref[...], preferred_element_type=f32
        )
        total = high + low
        top = total.astype(bf16)
        rest = (total - top.astype(f32)).astype(bf16)
        for order in range(3):
            lanes = slice(order * TESTS, (order + 1) * TESTS)
            rows = slice(order * TABLE + start, order * TABLE + start + size)
            table_ref[rows, :TESTS] = top[:, lanes]
            table_ref[rows, TESTS:] = rest[:, lanes]


def pick_table(codes_ref, keys_ref, pick_ref):
    for row in range(0, PICKED, 16):
        code = codes_ref[row // 128, row % 128 : row % 128 + 16, :]
        for column in range(0, KEYS, 128):
            width = min(128, KEYS - column)
            same = code[:, :width] == keys_ref[:, column : column + width]
            pick_ref[row : row + 16, column : column + width] = jnp.where(same, 1.0, 0.0).astype(
                bf16
            )


def whole_dot(left, right, contract):
    return lax.dot_general(
        left,
        right,
        (((1,), (contract,)), ((), ())),
        precision=lax.Precision.HIGHEST,
        preferred_element_type=f32,
    )


def solve(gram_ref, normal_ref, lib_ref, cross, target_squares, lib, coef_ref, fit_ref, spot_ref):
    total = float(ROWS)
    diagonal_row = []
    diagonal_column = []
    same = lax.broadcasted_iota(jnp.int32, (128, 128), 0) == lax.broadcasted_iota(
        jnp.int32, (128, 128), 1
    )
    for block in range(4):
        at = slice(block * 128, block * 128 + 128)
        spread = jnp.where(same, gram_ref[at, at], 0.0)
        diagonal_row.append(jnp.sum(spread, axis=0, keepdims=True))
        diagonal_column.append(jnp.sum(spread, axis=1, keepdims=True))
    inverse_row = [1.0 / jnp.sqrt(d / total + EPSILON) for d in diagonal_row]
    inverse_column = [1.0 / jnp.sqrt(d / total + EPSILON) for d in diagonal_column]
    for i in range(4):
        for j in range(4):
            rows, lanes = slice(i * 128, i * 128 + 128), slice(j * 128, j * 128 + 128)
            block = gram_ref[rows, lanes] * (inverse_column[i] / total) * inverse_row[j]
            if i == j:
                block = block + jnp.where(same, RIDGE, 0.0)
            high = block.astype(bf16)
            normal_ref[rows, lanes] = high
            normal_ref[rows, slice(TERMS + j * 128, TERMS + j * 128 + 128)] = (
                block - high.astype(f32)
            ).astype(bf16)
    inverse = jnp.concatenate(inverse_row, axis=1)
    target_scale = 1.0 / jnp.sqrt(target_squares / total + EPSILON)
    normal_cross = cross * inverse * (target_scale / total)

    def apply(rows):
        high = rows.astype(bf16)
        low = (rows - high.astype(f32)).astype(bf16)
        stacked = jnp.concatenate([high, low], axis=0)
        both = jnp.dot(stacked, normal_ref[...], preferred_element_type=f32)
        return both[:8, :TERMS] + both[:8, TERMS:] + both[8:, :TERMS]

    vector = jnp.full((8, TERMS), TERMS**-0.5, f32)
    magnitude = None
    for _ in range(POWER):
        applied = apply(vector)
        magnitude = jnp.sqrt(jnp.sum(applied * applied, axis=1, keepdims=True))
        vector = applied / magnitude
    step_size = 1.0 / magnitude
    bound = step_size * SHRINK
    coeffs = None
    for sweep in range(ITERS):
        if sweep == 0:
            moved = step_size * normal_cross
        else:
            moved = coeffs - step_size * (apply(coeffs) - normal_cross)
        coeffs = jnp.maximum(moved - bound, 0.0) - jnp.maximum(-moved - bound, 0.0)
    spot_ref[...] = coeffs
    own = pl.multiple_of(lib * 128, 128)
    coef_ref[...] = spot_ref[:, pl.ds(own, 128)][:4]
    fit_ref[...] = whole_dot(coeffs * inverse, lib_ref[:TERMS], 0)[:4]


def kernel(
    exponents_ref,
    code_weight_ref,
    keys_ref,
    start_ref,
    end_ref,
    plane_weight_ref,
    depth_weight_ref,
    coef_ref,
    fit_ref,
    fields_ref,
    later_ref,
    weights_ref,
    depth_ref,
    wide_ref,
    theta_ref,
    plane_ref,
    table_ref,
    codes_ref,
    pick_ref,
    edge_out_ref,
    edge_in_ref,
    lib_ref,
    gram_ref,
    half_ref,
    half_in_ref,
    part_ref,
    parts_in_ref,
    done_ref,
    other_ref,
    normal_ref,
    spot_ref,
    local_sems,
    code_sems,
    edge_sems,
    core_sems,
    part_sems,
    done_sems,
    other_sems,
):
    sub = lax.axis_index("sub")
    lib = lax.axis_index("lib")
    x, y, z, core = position()
    chip = (x * 4 + y) * 4 + z
    next_sub = {"sub": (sub + 1) % 32, "lib": lib}
    last_sub = {"sub": (sub + 31) % 32, "lib": lib}
    other_core = {"sub": sub, "lib": lib + 1 - 2 * core}
    window = pl.ds(pl.multiple_of(jnp.maximum(lib * 32 - 8, 0), 8), CELLS_Y)
    loads = [
        pltpu.make_async_copy(start_ref.at[:, :, window, :], fields_ref, local_sems.at[0]),
        pltpu.make_async_copy(end_ref.at[:, :, window, :], later_ref, local_sems.at[1]),
        pltpu.make_async_copy(
            plane_weight_ref.at[jnp.minimum(lib, 1)], weights_ref, local_sems.at[2]
        ),
        pltpu.make_async_copy(depth_weight_ref, depth_ref, local_sems.at[3]),
    ]
    for load in loads:
        load.start()

    barrier = pltpu.get_barrier_semaphore()

    def greet(step, carry):
        pl.semaphore_signal(
            barrier,
            inc=1,
            device_id=chip_device((chip + step) % CHIPS, core),
            device_id_type=MESH,
        )
        return carry

    lax.fori_loop(1, CHIPS, greet, 0)
    for device in (
        next_sub,
        last_sub,
        {"sub": sub, "lib": (lib + 1) % 4},
        {"sub": sub, "lib": (lib + 2) % 4},
        {"sub": sub, "lib": (lib + 3) % 4},
    ):
        pl.semaphore_signal(barrier, inc=1, device_id=device, device_id_type=MESH)

    code = jnp.sum(
        exponents_ref[...].astype(f32) * code_weight_ref[...], axis=1, keepdims=True
    )
    codes_ref[lib] = jnp.broadcast_to(code, (128, 128))
    row = lax.broadcasted_iota(jnp.int32, (16, 128), 0)
    codes_ref[4, :16, :] = jnp.where(row < 4, TARGET_CODE + row, -1).astype(f32)

    pl.semaphore_wait(barrier, CHIPS - 1 + 5)
    code_copies = [
        pltpu.make_async_remote_copy(
            src_ref=codes_ref.at[lib],
            dst_ref=codes_ref.at[lib],
            send_sem=code_sems.at[step],
            recv_sem=code_sems.at[3 + step],
            device_id={"sub": sub, "lib": (lib + 1 + step) % 4},
            device_id_type=MESH,
        )
        for step in range(3)
    ]
    for copy in code_copies:
        copy.start()

    loads[0].wait()
    loads[1].wait()
    products(fields_ref, later_ref, wide_ref, theta_ref)
    loads[2].wait()
    plane_sums(weights_ref, theta_ref, plane_ref)
    loads[3].wait()
    depth_sums(plane_ref, depth_ref, table_ref.at[1], 1)
    for copy in code_copies:
        copy.wait()
    pick_table(codes_ref, keys_ref, pick_ref)
    both = jnp.dot(pick_ref[...], table_ref[1], preferred_element_type=f32)
    edge_out_ref[...] = (both[:, :TESTS] + both[:, TESTS:]).astype(bf16)
    edge = pltpu.make_async_remote_copy(
        src_ref=edge_out_ref,
        dst_ref=edge_in_ref,
        send_sem=edge_sems.at[0],
        recv_sem=edge_sems.at[1],
        device_id=next_sub,
        device_id_type=MESH,
    )
    edge.start()
    depth_sums(plane_ref, depth_ref, table_ref.at[0], 0)
    both = jnp.dot(pick_ref[...], table_ref[0], preferred_element_type=f32)
    lib_ref[...] = both[:, :TESTS] + both[:, TESTS:]
    edge.wait()
    keep = jnp.where(sub > 0, 1.0, 0.0).astype(f32)
    lib_ref[...] = lib_ref[...] + keep * edge_in_ref[...].astype(f32)

    library = lib_ref[:TERMS]
    gram_ref[...] = whole_dot(library, library, 1)
    target = lib_ref[TERMS : TERMS + 8]
    cross = whole_dot(target, library, 1)
    squares = jnp.broadcast_to(jnp.sum(target * target, axis=1, keepdims=True), (8, 128))

    for half in range(2):
        for number, (i, j) in enumerate(BLOCKS[half]):
            for part in range(8):
                half_ref[half, number * 8 + part] = gram_ref[
                    i * 128 + part * 16 : i * 128 + part * 16 + 16, j * 128 : j * 128 + 128
                ]
    for block in range(4):
        half_ref[0, CHUNKS - 1, block * 4 : block * 4 + 4, :] = cross[
            :4, block * 128 : block * 128 + 128
        ]
    half_ref[1, CHUNKS - 1, :8, :] = squares
    half_ref[1, CHUNKS - 1, 8:, :] = jnp.zeros((8, 128), f32)

    pair = pltpu.make_async_remote_copy(
        src_ref=half_ref.at[1 - core],
        dst_ref=half_in_ref,
        send_sem=core_sems.at[0],
        recv_sem=core_sems.at[1],
        device_id=other_core,
        device_id_type=MESH,
    )
    pair.start()
    pair.wait()
    part_ref[...] = half_ref[core] + half_in_ref[...]

    mine = (chip * UNSPREAD) % CHIPS
    owner = mine < CHUNKS

    def give(step, carry):
        chunk = (mine + step) % CHUNKS
        to = (chunk * SPREAD) % CHIPS

        @pl.when(to != chip)
        def _():
            pltpu.make_async_remote_copy(
                src_ref=part_ref.at[chunk],
                dst_ref=parts_in_ref.at[chip],
                send_sem=part_sems.at[0],
                recv_sem=part_sems.at[1],
                device_id=chip_device(to, core),
                device_id_type=MESH,
            ).start()

        return carry

    lax.fori_loop(0, CHUNKS, give, 0)

    @pl.when(owner)
    def _():
        own = parts_in_ref.at[pl.ds(0, CHIPS - 1)]
        pltpu.make_async_copy(own, own, part_sems.at[1]).wait()
        parts_in_ref[chip] = part_ref[mine]
        done_ref[mine] = jnp.sum(parts_in_ref[...], axis=0)

        def show(step, carry):
            pltpu.make_async_remote_copy(
                src_ref=done_ref.at[mine],
                dst_ref=done_ref.at[mine],
                send_sem=done_sems.at[0],
                recv_sem=done_sems.at[1],
                device_id=chip_device((chip + step) % CHIPS, core),
                device_id_type=MESH,
            ).start()
            return carry

        lax.fori_loop(1, CHIPS, show, 0)
        sent = parts_in_ref.at[pl.ds(0, CHIPS - 1)]
        pltpu.make_async_copy(sent, sent, done_sems.at[0]).wait()
        rest = part_ref.at[pl.ds(0, CHUNKS - 1)]
        pltpu.make_async_copy(rest, rest, part_sems.at[0]).wait()
        pltpu.make_async_copy(rest, rest, done_sems.at[1]).wait()

    @pl.when(jnp.logical_not(owner))
    def _():
        pltpu.make_async_copy(part_ref, part_ref, part_sems.at[0]).wait()
        pltpu.make_async_copy(part_ref, part_ref, done_sems.at[1]).wait()

    swap = pltpu.make_async_remote_copy(
        src_ref=done_ref,
        dst_ref=other_ref,
        send_sem=other_sems.at[0],
        recv_sem=other_sems.at[1],
        device_id=other_core,
        device_id_type=MESH,
    )
    swap.start()
    swap.wait()
    half_ref[core] = done_ref[...]
    half_ref[1 - core] = other_ref[...]

    for half in range(2):
        for number, (i, j) in enumerate(BLOCKS[half]):
            for part in range(8):
                gram_ref[
                    i * 128 + part * 16 : i * 128 + part * 16 + 16, j * 128 : j * 128 + 128
                ] = half_ref[half, number * 8 + part]
    for i in range(4):
        for j in range(i):
            gram_ref[i * 128 : i * 128 + 128, j * 128 : j * 128 + 128] = gram_ref[
                j * 128 : j * 128 + 128, i * 128 : i * 128 + 128
            ].T
    cross_sum = jnp.concatenate(
        [
            jnp.concatenate(
                [half_ref[0, CHUNKS - 1, block * 4 : block * 4 + 4, :] for block in range(4)],
                axis=1,
            ),
            jnp.zeros((4, TERMS), f32),
        ],
        axis=0,
    )
    square_sum = half_ref[1, CHUNKS - 1, :8, :1]
    solve(
        gram_ref, normal_ref, lib_ref, cross_sum, square_sum, lib, coef_ref, fit_ref, spot_ref
    )


def local(snap_start, snap_end, exponents):
    vmem = pl.BlockSpec(memory_space=pltpu.VMEM)
    anywhere = pl.BlockSpec(memory_space=pl.ANY)
    return pl.pallas_call(
        kernel,
        out_shape=(
            jax.ShapeDtypeStruct((4, TERMS // 4), f32),
            jax.ShapeDtypeStruct((4, TESTS), f32),
        ),
        in_specs=[vmem, vmem, vmem, anywhere, anywhere, anywhere, anywhere],
        out_specs=(vmem, vmem),
        scratch_shapes=[
            pltpu.VMEM((4, CELLS_X, CELLS_Y, WIDTH_Z), bf16),
            pltpu.VMEM((4, CELLS_X, CELLS_Y, WIDTH_Z), bf16),
            pltpu.VMEM((4 * CENTERS_Y * PAD, CELLS_XY), bf16),
            pltpu.VMEM((CENTERS_Y * WIDTH_Z, 3 * TESTS), bf16),
            pltpu.VMEM((8, CELLS_XY, WIDTH_Z), f32),
            pltpu.VMEM((PRODUCTS, CELLS_XY, WIDTH_Z), bf16),
            pltpu.VMEM((2, 2, TABLE, CENTERS_Y * WIDTH_Z), bf16),
            pltpu.VMEM((2, KEYS, 2 * TESTS), bf16),
            pltpu.VMEM((5, 128, 128), f32),
            pltpu.VMEM((PICKED, KEYS), bf16),
            pltpu.VMEM((PICKED, TESTS), bf16),
            pltpu.VMEM((PICKED, TESTS), bf16),
            pltpu.VMEM((PICKED, TESTS), f32),
            pltpu.VMEM((TERMS, TERMS), f32),
            pltpu.VMEM((2, CHUNKS, CHUNK, 128), f32),
            pltpu.VMEM((CHUNKS, CHUNK, 128), f32),
            pltpu.VMEM((CHUNKS, CHUNK, 128), f32),
            pltpu.VMEM((CHIPS, CHUNK, 128), f32),
            pltpu.VMEM((CHUNKS, CHUNK, 128), f32),
            pltpu.VMEM((CHUNKS, CHUNK, 128), f32),
            pltpu.VMEM((TERMS, 2 * TERMS), bf16),
            pltpu.VMEM((8, TERMS), f32),
            pltpu.SemaphoreType.DMA((4,)),
            pltpu.SemaphoreType.DMA((6,)),
            pltpu.SemaphoreType.DMA((2,)),
            pltpu.SemaphoreType.DMA((2,)),
            pltpu.SemaphoreType.DMA((2,)),
            pltpu.SemaphoreType.DMA((2,)),
            pltpu.SemaphoreType.DMA((2,)),
        ],
        compiler_params=pltpu.CompilerParams(
            collective_id=0, has_side_effects=True, vmem_limit_bytes=56 << 20
        ),
        name="weak_form_fit",
    )(
        exponents,
        jnp.asarray(code_weights()),
        jnp.asarray(column_codes()),
        snap_start,
        snap_end,
        jnp.asarray(plane_weights()),
        jnp.asarray(depth_weights()),
    )


def solution(mesh):
    placed = (P(None, "sub", None, None), P(None, "sub", None, None), P("lib", None))
    return jax.shard_map(
        local,
        mesh=mesh,
        in_specs=placed,
        out_specs=(P(None, "lib"), P(None, ("sub", "lib"))),
        check_vma=False,
    )
```

time: 1000 us -> 61.3 us (0.06)
  waiting for transfers between devices: 420 us -> 0 us
  matrix products: 259 us -> 0 us
  blocking collectives: 198 us -> 0 us
  other arithmetic: 79.8 us -> 0 us
  Pallas kernels: 0 us -> 56.5 us
  between operations: 18.6 us -> 0.64 us
    psum x1 -> x0, waiting for transfers between devices: 334 us -> none  [local(): lax.psum((gram_rows, squares, cross_terms, target_squares), 'sub')]
    dot_general x120 -> x0, matrix products: 258 us -> none  [the longest x17 122 us: weak_block(): jnp.einsum('txyc,tyb->txbc', reduced, select_taps(y_table, orders[:, 1]),...]
    all_gather x17 -> x0, blocking collectives: 113 us -> none  [the longest x6 52.5 us: local(): lax.all_gather(jnp.dot(normal_rows, vector, precision=highest), 'lib', ax...]
    psum x1 -> x0, blocking collectives: 85.1 us -> none  [local(): lax.psum((gram_rows, squares, cross_terms, target_squares), 'sub')]
    broadcast_in_dim x33 -> x0, other arithmetic: 69.6 us -> none  [the longest x32 69.6 us: monomial_block(): jnp.where(power_here == 1, values, values * values)]
    ppermute x2 -> x0, waiting for transfers between devices: 68.9 us -> none  [shifted(): lax.ppermute(value, axis, [(source, source + steps) for source in range(f...]
    pallas_call x0 -> x1, Pallas kernels: none -> 56.5 us  [local(): pl.pallas_call(kernel, out_shape=(jax.ShapeDtypeStruct((4, TERMS // 4), f...]
    unnamed x3 -> x0, waiting for transfers between devices: 17.7 us -> none
  transfers between devices with their start and end apart: 4 -> 0, of which waited for: 4 -> 0; matrix products, arithmetic and copies ran while one was open for 0% -> 0% of each run, Pallas kernels for 0% -> 0%
where the time goes in v1:
time: 61.3 us; the launch traced here: 61.1 us
  Pallas kernels  56.5 us (92%)
  local copies, waits for them, and re-layouts  3.92 us (6%)
  between operations  0.64 us (1%)
    pallas_call x1, Pallas kernels, local(): pl.pallas_call(kernel, out_shape=(jax.ShapeDtypeStruct((4, TERMS // 4), f...  56.5 us
    unnamed x3, local copies, waits for them, and re-layouts  3.92 us

profile of v1, /device:TPU:1, one launch (start us, length us, event | category | flops | bytes accessed | tf_op | source)
XLA Modules:
  0.0 61.1 jit_solution(3441420432847589283)
XLA Ops:
  0.6 1.4 %copy.9.exponents_ref = s32[128,7]{1,0:T(8,128)} copy(s32[128,7]{0,1:T(8,128)} %param.9) | data formatting | bytes 7168 | tf_op args[2]
  2.0 56.5 %weak_form_fit.1 = (f32[4,128]{1,0:T(4,128)}, f32[4,128]{1,0:T(4,128)}) custom-call(s32[128,7]{1,0:T(8,128)} %copy.9.exponents_ref, f32[1,7]{1,0:T(1,128)} %constant.8.clone.code_weight_ref, f32[1,1632]{1,0:T(1,128)} %constant.9.clone.keys_ref, bf16[4,8,128,256]{3,2,1,0:T(8,128)(2,1)} %start_ref.1, bf16[4,8,128,256]{3,2,1,0:T(8,128)(2,1)} %end_ref.1, ...), custom_call_target="tpu_custom_call" | custom-call | tf_op jit(solution)/shard_map/weak_form_fit/pallas_call | solution.py:539
  58.6 1.2 %copy.12 = f32[4,128]{1,0:T(4,128)} copy(f32[4,128]{1,0:T(4,128)} %get-tuple-element.4) | data formatting | bytes 4096
  59.8 1.3 %copy.13 = f32[4,128]{1,0:T(4,128)} copy(f32[4,128]{1,0:T(4,128)} %get-tuple-element.5) | data formatting | bytes 4096

commit v2 on v1

--- a/solution.py
+++ b/solution.py
@@ -42,15 +42,16 @@
 PICKED = TERMS + 16
 TARGET_CODE = 4000
 
-CHUNK = 16
+CHUNK = 10
+CHIPS = 64
 BLOCKS = (
     ((0, 0), (0, 1), (0, 2), (0, 3), (3, 3)),
     ((1, 1), (1, 2), (1, 3), (2, 2), (2, 3)),
 )
-CHUNKS = 8 * len(BLOCKS[0]) + 1
-CHIPS = 64
-SPREAD = 25
-UNSPREAD = 41
+HOPS = (0, 1, 2, 1)
+PARTNERS = sorted(
+    range(1, CHIPS), key=lambda d: -(HOPS[d // 16] + HOPS[d // 4 % 4] + HOPS[d % 4])
+)
 
 MESH = pl.DeviceIdType.MESH
 f32 = jnp.float32
@@ -83,8 +84,8 @@
                         full[side, center, order_x * 3 + order_y] = tap(
                             order_x, x - STRIDE * side
                         ) * tap(order_y, y - STRIDE * center - shift)
-        high, low = split_pieces(full.reshape(2 * CENTERS_Y * PAD, CELLS_XY))
-        both.append(np.concatenate([high, low]))
+        high, low = split_pieces(full.reshape(2, CENTERS_Y * PAD, CELLS_XY))
+        both.append(np.concatenate([high, low], axis=1))
     return np.stack(both)
 
 
@@ -112,18 +113,34 @@
 
 
 def code_weights():
-    return np.array([[729, 243, 81, 27, 9, 3, 1]], np.float32)
-
-
-def position():
-    sub = lax.axis_index("sub")
-    lib = lax.axis_index("lib")
-    return sub // 8, (sub // 4) % 2 * 2 + lib // 2, sub % 4, lib % 2
-
-
-def chip_device(chip, core):
-    y = chip // 4 % 4
-    return {"sub": (chip // 16 * 2 + y // 2) * 4 + chip % 4, "lib": y % 2 * 2 + core}
+    return np.array([[729], [243], [81], [27], [9], [3], [1]], np.float32)
+
+
+def others(value):
+    return value, value + 1 - 2 * (value % 2), (value + 2) % 4, 3 - value
+
+
+class Chips:
+    def __init__(self):
+        sub = lax.axis_index("sub")
+        lib = lax.axis_index("lib")
+        self.core = lib % 2
+        self.x = others(sub // 8)
+        self.y = others((sub // 4) % 2 * 2 + lib // 2)
+        self.z = others(sub % 4)
+        self.sub_x = [8 * v for v in self.x]
+        self.sub_y = [v // 2 * 4 for v in self.y]
+        self.lib_y = [v % 2 * 2 + self.core for v in self.y]
+        self.chip_xy = [[16 * v + 4 * w for w in self.y] for v in self.x]
+
+    def chip(self, d):
+        return self.chip_xy[d // 16][d // 4 % 4] + self.z[d % 4]
+
+    def device(self, d):
+        return {
+            "sub": self.sub_x[d // 16] + self.sub_y[d // 4 % 4] + self.z[d % 4],
+            "lib": self.lib_y[d // 4 % 4],
+        }
 
 
 def products(fields_ref, later_ref, wide_ref, theta_ref):
@@ -136,7 +153,12 @@
 
     def rows(step, carry):
         at = pl.multiple_of(step * 16, 16)
-        value = [wide_ref[field, pl.ds(at, 16), :] for field in range(4)]
+        for half in range(2):
+            some(at, slice(half * 128, half * 128 + 128))
+        return carry
+
+    def some(at, lanes):
+        value = [wide_ref[field, pl.ds(at, 16), lanes] for field in range(4)]
         square = [v * v for v in value]
         pairs = {}
         for index, powers in enumerate(POWERS):
@@ -154,33 +176,31 @@
                 else:
                     result = result * factor
                     pairs[key] = result
-            theta_ref[index, pl.ds(at, 16), :] = result.astype(bf16)
+            theta_ref[index, pl.ds(at, 16), lanes] = result.astype(bf16)
         for field in range(4):
-            change = wide_ref[4 + field, pl.ds(at, 16), :] - value[field]
-            theta_ref[len(POWERS) + field, pl.ds(at, 16), :] = change.astype(bf16)
-        return carry
+            change = wide_ref[4 + field, pl.ds(at, 16), lanes] - value[field]
+            theta_ref[len(POWERS) + field, pl.ds(at, 16), lanes] = change.astype(bf16)
 
     lax.fori_loop(0, CELLS_XY // 16, rows, 0)
 
 
-def plane_sums(weights_ref, theta_ref, plane_ref):
-    half = 2 * CENTERS_Y * PAD
+def plane_sums(weights_ref, theta_ref, plane_ref, side):
+    half = CENTERS_Y * PAD
 
     def one(index, carry):
-        both = jnp.dot(weights_ref[...], theta_ref[index], preferred_element_type=f32)
+        both = jnp.dot(weights_ref[side], theta_ref[index], preferred_element_type=f32)
         total = both[:half] + both[half:]
         high = total.astype(bf16)
         low = (total - high.astype(f32)).astype(bf16)
         at = pl.multiple_of(index * PAD, PAD)
-        for side in range(2):
-            for center in range(CENTERS_Y):
-                row = (side * CENTERS_Y + center) * PAD
-                lanes = slice(center * WIDTH_Z, (center + 1) * WIDTH_Z)
-                plane_ref[side, 0, pl.ds(at, PAD), lanes] = high[row : row + PAD]
-                plane_ref[side, 1, pl.ds(at, PAD), lanes] = low[row : row + PAD]
+        for center in range(CENTERS_Y):
+            row = center * PAD
+            lanes = slice(center * WIDTH_Z, (center + 1) * WIDTH_Z)
+            plane_ref[side, 0, pl.ds(at, PAD), lanes] = high[row : row + PAD]
+            plane_ref[side, 1, pl.ds(at, PAD), lanes] = low[row : row + PAD]
         return carry
 
-    lax.fori_loop(0, PRODUCTS, one, 0)
+    lax.fori_loop(0, PRODUCTS, one, 0, unroll=2)
 
 
 def depth_sums(plane_ref, depth_ref, table_ref, side):
@@ -223,7 +243,7 @@
     )
 
 
-def solve(gram_ref, normal_ref, lib_ref, cross, target_squares, lib, coef_ref, fit_ref, spot_ref):
+def solve(gram_ref, normal_ref, lib_ref, cross, target_squares, lib, result_ref, spot_ref):
     total = float(ROWS)
     diagonal_row = []
     diagonal_column = []
@@ -260,12 +280,12 @@
         return both[:8, :TERMS] + both[:8, TERMS:] + both[8:, :TERMS]
 
     vector = jnp.full((8, TERMS), TERMS**-0.5, f32)
-    magnitude = None
-    for _ in range(POWER):
-        applied = apply(vector)
-        magnitude = jnp.sqrt(jnp.sum(applied * applied, axis=1, keepdims=True))
-        vector = applied / magnitude
-    step_size = 1.0 / magnitude
+    for _ in range(POWER - 1):
+        vector = apply(vector)
+    applied = apply(vector)
+    before = jnp.sum(vector * vector, axis=1, keepdims=True)
+    after = jnp.sum(applied * applied, axis=1, keepdims=True)
+    step_size = jnp.sqrt(before) / jnp.sqrt(after)
     bound = step_size * SHRINK
     coeffs = None
     for sweep in range(ITERS):
@@ -276,8 +296,8 @@
         coeffs = jnp.maximum(moved - bound, 0.0) - jnp.maximum(-moved - bound, 0.0)
     spot_ref[...] = coeffs
     own = pl.multiple_of(lib * 128, 128)
-    coef_ref[...] = spot_ref[:, pl.ds(own, 128)][:4]
-    fit_ref[...] = whole_dot(coeffs * inverse, lib_ref[:TERMS], 0)[:4]
+    result_ref[:8, :] = spot_ref[:, pl.ds(own, 128)]
+    result_ref[8:, :] = whole_dot(coeffs * inverse, lib_ref[:TERMS], 0)
 
 
 def kernel(
@@ -288,8 +308,7 @@
     end_ref,
     plane_weight_ref,
     depth_weight_ref,
-    coef_ref,
-    fit_ref,
+    result_ref,
     fields_ref,
     later_ref,
     weights_ref,
@@ -306,10 +325,8 @@
     gram_ref,
     half_ref,
     half_in_ref,
-    part_ref,
     parts_in_ref,
     done_ref,
-    other_ref,
     normal_ref,
     spot_ref,
     local_sems,
@@ -322,8 +339,8 @@
 ):
     sub = lax.axis_index("sub")
     lib = lax.axis_index("lib")
-    x, y, z, core = position()
-    chip = (x * 4 + y) * 4 + z
+    chips = Chips()
+    core = chips.core
     next_sub = {"sub": (sub + 1) % 32, "lib": lib}
     last_sub = {"sub": (sub + 31) % 32, "lib": lib}
     other_core = {"sub": sub, "lib": lib + 1 - 2 * core}
@@ -341,16 +358,8 @@
 
     barrier = pltpu.get_barrier_semaphore()
 
-    def greet(step, carry):
-        pl.semaphore_signal(
-            barrier,
-            inc=1,
-            device_id=chip_device((chip + step) % CHIPS, core),
-            device_id_type=MESH,
-        )
-        return carry
-
-    lax.fori_loop(1, CHIPS, greet, 0)
+    for d in PARTNERS:
+        pl.semaphore_signal(barrier, inc=1, device_id=chips.device(d), device_id_type=MESH)
     for device in (
         next_sub,
         last_sub,
@@ -361,12 +370,15 @@
         pl.semaphore_signal(barrier, inc=1, device_id=device, device_id_type=MESH)
 
     code = jnp.sum(
-        exponents_ref[...].astype(f32) * code_weight_ref[...], axis=1, keepdims=True
-    )
-    codes_ref[lib] = jnp.broadcast_to(code, (128, 128))
+        exponents_ref[...].astype(f32) * code_weight_ref[...], axis=0, keepdims=True
+    )
+    codes_ref[lib] = jnp.broadcast_to(code, (128, 128)).T
     row = lax.broadcasted_iota(jnp.int32, (16, 128), 0)
     codes_ref[4, :16, :] = jnp.where(row < 4, TARGET_CODE + row, -1).astype(f32)
 
+    loads[0].wait()
+    loads[1].wait()
+    products(fields_ref, later_ref, wide_ref, theta_ref)
     pl.semaphore_wait(barrier, CHIPS - 1 + 5)
     code_copies = [
         pltpu.make_async_remote_copy(
@@ -381,17 +393,13 @@
     ]
     for copy in code_copies:
         copy.start()
-
-    loads[0].wait()
-    loads[1].wait()
-    products(fields_ref, later_ref, wide_ref, theta_ref)
     loads[2].wait()
-    plane_sums(weights_ref, theta_ref, plane_ref)
-    loads[3].wait()
-    depth_sums(plane_ref, depth_ref, table_ref.at[1], 1)
+    plane_sums(weights_ref, theta_ref, plane_ref, 1)
     for copy in code_copies:
         copy.wait()
     pick_table(codes_ref, keys_ref, pick_ref)
+    loads[3].wait()
+    depth_sums(plane_ref, depth_ref, table_ref.at[1], 1)
     both = jnp.dot(pick_ref[...], table_ref[1], preferred_element_type=f32)
     edge_out_ref[...] = (both[:, :TESTS] + both[:, TESTS:]).astype(bf16)
     edge = pltpu.make_async_remote_copy(
@@ -403,6 +411,7 @@
         device_id_type=MESH,
     )
     edge.start()
+    plane_sums(weights_ref, theta_ref, plane_ref, 0)
     depth_sums(plane_ref, depth_ref, table_ref.at[0], 0)
     both = jnp.dot(pick_ref[...], table_ref[0], preferred_element_type=f32)
     lib_ref[...] = both[:, :TESTS] + both[:, TESTS:]
@@ -416,19 +425,20 @@
     cross = whole_dot(target, library, 1)
     squares = jnp.broadcast_to(jnp.sum(target * target, axis=1, keepdims=True), (8, 128))
 
+    for piece in range(8):
+        gram_ref[64 + piece * 4 : 68 + piece * 4, :64] = cross[:4, piece * 64 : piece * 64 + 64]
+    gram_ref[96:100, :64] = squares[:4, :64]
+
     for half in range(2):
-        for number, (i, j) in enumerate(BLOCKS[half]):
-            for part in range(8):
-                half_ref[half, number * 8 + part] = gram_ref[
-                    i * 128 + part * 16 : i * 128 + part * 16 + 16, j * 128 : j * 128 + 128
-                ]
-    for block in range(4):
-        half_ref[0, CHUNKS - 1, block * 4 : block * 4 + 4, :] = cross[
-            :4, block * 128 : block * 128 + 128
-        ]
-    half_ref[1, CHUNKS - 1, :8, :] = squares
-    half_ref[1, CHUNKS - 1, 8:, :] = jnp.zeros((8, 128), f32)
-
+        for number, (i, j) in enumerate(BLOCKS[half][:4]):
+            lanes = slice(j * 128, j * 128 + 128)
+            for part in range(16):
+                row = i * 128 + part * 8
+                half_ref[half, number * 16 + part, :8, :] = gram_ref[row : row + 8, lanes]
+        i, j = BLOCKS[half][4]
+        for part in range(CHIPS):
+            row = i * 128 + part * 2
+            half_ref[half, part, 8:, :] = gram_ref[row : row + 2, j * 128 : j * 128 + 128]
     pair = pltpu.make_async_remote_copy(
         src_ref=half_ref.at[1 - core],
         dst_ref=half_in_ref,
@@ -439,63 +449,36 @@
     )
     pair.start()
     pair.wait()
-    part_ref[...] = half_ref[core] + half_in_ref[...]
-
-    mine = (chip * UNSPREAD) % CHIPS
-    owner = mine < CHUNKS
-
-    def give(step, carry):
-        chunk = (mine + step) % CHUNKS
-        to = (chunk * SPREAD) % CHIPS
-
-        @pl.when(to != chip)
-        def _():
-            pltpu.make_async_remote_copy(
-                src_ref=part_ref.at[chunk],
-                dst_ref=parts_in_ref.at[chip],
-                send_sem=part_sems.at[0],
-                recv_sem=part_sems.at[1],
-                device_id=chip_device(to, core),
-                device_id_type=MESH,
-            ).start()
-
-        return carry
-
-    lax.fori_loop(0, CHUNKS, give, 0)
-
-    @pl.when(owner)
-    def _():
-        own = parts_in_ref.at[pl.ds(0, CHIPS - 1)]
-        pltpu.make_async_copy(own, own, part_sems.at[1]).wait()
-        parts_in_ref[chip] = part_ref[mine]
-        done_ref[mine] = jnp.sum(parts_in_ref[...], axis=0)
-
-        def show(step, carry):
-            pltpu.make_async_remote_copy(
-                src_ref=done_ref.at[mine],
-                dst_ref=done_ref.at[mine],
-                send_sem=done_sems.at[0],
-                recv_sem=done_sems.at[1],
-                device_id=chip_device((chip + step) % CHIPS, core),
-                device_id_type=MESH,
-            ).start()
-            return carry
-
-        lax.fori_loop(1, CHIPS, show, 0)
-        sent = parts_in_ref.at[pl.ds(0, CHIPS - 1)]
-        pltpu.make_async_copy(sent, sent, done_sems.at[0]).wait()
-        rest = part_ref.at[pl.ds(0, CHUNKS - 1)]
-        pltpu.make_async_copy(rest, rest, part_sems.at[0]).wait()
-        pltpu.make_async_copy(rest, rest, done_sems.at[1]).wait()
-
-    @pl.when(jnp.logical_not(owner))
-    def _():
-        pltpu.make_async_copy(part_ref, part_ref, part_sems.at[0]).wait()
-        pltpu.make_async_copy(part_ref, part_ref, done_sems.at[1]).wait()
-
+    half_in_ref[...] = half_in_ref[...] + half_ref[core]
+    own = chips.chip(0)
+    for d in PARTNERS:
+        pltpu.make_async_remote_copy(
+            src_ref=half_in_ref.at[chips.chip(d)],
+            dst_ref=parts_in_ref.at[d],
+            send_sem=part_sems.at[0],
+            recv_sem=part_sems.at[1],
+            device_id=chips.device(d),
+            device_id_type=MESH,
+        ).start()
+    parts_in_ref[0] = half_in_ref[own]
+    received = parts_in_ref.at[pl.ds(1, CHIPS - 1)]
+    pltpu.make_async_copy(received, received, part_sems.at[1]).wait()
+    done_ref[core, own] = jnp.sum(parts_in_ref[...], axis=0)
+    for d in PARTNERS:
+        pltpu.make_async_remote_copy(
+            src_ref=done_ref.at[core, own],
+            dst_ref=done_ref.at[core, own],
+            send_sem=done_sems.at[0],
+            recv_sem=done_sems.at[1],
+            device_id=chips.device(d),
+            device_id_type=MESH,
+        ).start()
+    pltpu.make_async_copy(received, received, part_sems.at[0]).wait()
+    pltpu.make_async_copy(received, received, done_sems.at[1]).wait()
+    pltpu.make_async_copy(received, received, done_sems.at[0]).wait()
     swap = pltpu.make_async_remote_copy(
-        src_ref=done_ref,
-        dst_ref=other_ref,
+        src_ref=done_ref.at[core],
+        dst_ref=done_ref.at[core],
         send_sem=other_sems.at[0],
         recv_sem=other_sems.at[1],
         device_id=other_core,
@@ -503,51 +486,54 @@
     )
     swap.start()
     swap.wait()
-    half_ref[core] = done_ref[...]
-    half_ref[1 - core] = other_ref[...]
-
     for half in range(2):
-        for number, (i, j) in enumerate(BLOCKS[half]):
-            for part in range(8):
-                gram_ref[
-                    i * 128 + part * 16 : i * 128 + part * 16 + 16, j * 128 : j * 128 + 128
-                ] = half_ref[half, number * 8 + part]
+        for number, (i, j) in enumerate(BLOCKS[half][:4]):
+            lanes = slice(j * 128, j * 128 + 128)
+            for part in range(16):
+                row = i * 128 + part * 8
+                gram_ref[row : row + 8, lanes] = done_ref[half, number * 16 + part, :8, :]
+        i, j = BLOCKS[half][4]
+        for part in range(CHIPS):
+            row = i * 128 + part * 2
+            gram_ref[row : row + 2, j * 128 : j * 128 + 128] = done_ref[half, part, 8:, :]
+    cross_sum = jnp.concatenate(
+        [
+            jnp.concatenate(
+                [gram_ref[64 + piece * 4 : 68 + piece * 4, :64] for piece in range(8)], axis=1
+            ),
+            jnp.zeros((4, TERMS), f32),
+        ],
+        axis=0,
+    )
+    square_sum = jnp.concatenate([gram_ref[96:100, :1], jnp.zeros((4, 1), f32)], axis=0)
+    gram_ref[64:128, :64] = gram_ref[:64, 64:128].T
     for i in range(4):
         for j in range(i):
             gram_ref[i * 128 : i * 128 + 128, j * 128 : j * 128 + 128] = gram_ref[
                 j * 128 : j * 128 + 128, i * 128 : i * 128 + 128
             ].T
-    cross_sum = jnp.concatenate(
-        [
-            jnp.concatenate(
-                [half_ref[0, CHUNKS - 1, block * 4 : block * 4 + 4, :] for block in range(4)],
-                axis=1,
-            ),
-            jnp.zeros((4, TERMS), f32),
-        ],
-        axis=0,
-    )
-    square_sum = half_ref[1, CHUNKS - 1, :8, :1]
     solve(
-        gram_ref, normal_ref, lib_ref, cross_sum, square_sum, lib, coef_ref, fit_ref, spot_ref
-    )
+        gram_ref, normal_ref, lib_ref, cross_sum, square_sum, lib, result_ref, spot_ref
+    )
+
+
+def split_result(result_ref, coef_ref, fit_ref):
+    coef_ref[...] = result_ref[:4]
+    fit_ref[...] = result_ref[8:12]
 
 
 def local(snap_start, snap_end, exponents):
     vmem = pl.BlockSpec(memory_space=pltpu.VMEM)
     anywhere = pl.BlockSpec(memory_space=pl.ANY)
-    return pl.pallas_call(
+    result = pl.pallas_call(
         kernel,
-        out_shape=(
-            jax.ShapeDtypeStruct((4, TERMS // 4), f32),
-            jax.ShapeDtypeStruct((4, TESTS), f32),
-        ),
+        out_shape=jax.ShapeDtypeStruct((16, TESTS), f32),
         in_specs=[vmem, vmem, vmem, anywhere, anywhere, anywhere, anywhere],
-        out_specs=(vmem, vmem),
+        out_specs=vmem,
         scratch_shapes=[
             pltpu.VMEM((4, CELLS_X, CELLS_Y, WIDTH_Z), bf16),
             pltpu.VMEM((4, CELLS_X, CELLS_Y, WIDTH_Z), bf16),
-            pltpu.VMEM((4 * CENTERS_Y * PAD, CELLS_XY), bf16),
+            pltpu.VMEM((2, 2 * CENTERS_Y * PAD, CELLS_XY), bf16),
             pltpu.VMEM((CENTERS_Y * WIDTH_Z, 3 * TESTS), bf16),
             pltpu.VMEM((8, CELLS_XY, WIDTH_Z), f32),
             pltpu.VMEM((PRODUCTS, CELLS_XY, WIDTH_Z), bf16),
@@ -559,12 +545,10 @@
             pltpu.VMEM((PICKED, TESTS), bf16),
             pltpu.VMEM((PICKED, TESTS), f32),
             pltpu.VMEM((TERMS, TERMS), f32),
-            pltpu.VMEM((2, CHUNKS, CHUNK, 128), f32),
-            pltpu.VMEM((CHUNKS, CHUNK, 128), f32),
-            pltpu.VMEM((CHUNKS, CHUNK, 128), f32),
+            pltpu.VMEM((2, CHIPS, CHUNK, 128), f32),
             pltpu.VMEM((CHIPS, CHUNK, 128), f32),
-            pltpu.VMEM((CHUNKS, CHUNK, 128), f32),
-            pltpu.VMEM((CHUNKS, CHUNK, 128), f32),
+            pltpu.VMEM((CHIPS, CHUNK, 128), f32),
+            pltpu.VMEM((2, CHIPS, CHUNK, 128), f32),
             pltpu.VMEM((TERMS, 2 * TERMS), bf16),
             pltpu.VMEM((8, TERMS), f32),
             pltpu.SemaphoreType.DMA((4,)),
@@ -580,7 +564,7 @@
         ),
         name="weak_form_fit",
     )(
-        exponents,
+        exponents.T,
         jnp.asarray(code_weights()),
         jnp.asarray(column_codes()),
         snap_start,
@@ -588,6 +572,16 @@
         jnp.asarray(plane_weights()),
         jnp.asarray(depth_weights()),
     )
+    return pl.pallas_call(
+        split_result,
+        out_shape=(
+            jax.ShapeDtypeStruct((4, TERMS // 4), f32),
+            jax.ShapeDtypeStruct((4, TESTS), f32),
+        ),
+        in_specs=[vmem],
+        out_specs=(vmem, vmem),
+        name="split_result",
+    )(result)
 
 
 def solution(mesh):

time: 61.3 us -> 50.5 us (0.82)
  Pallas kernels: 56.5 us -> 49.6 us
  local copies, waits for them, and re-layouts: 3.92 us -> 0 us
    pallas_call x1 -> x2, Pallas kernels: 56.5 us -> 49.6 us  [the longest x1 48.3 us: local(): pl.pallas_call(kernel, out_shape=jax.ShapeDtypeStruct((16, TESTS), f32),...]
    unnamed x3 -> x0, local copies, waits for them, and re-layouts: 3.92 us -> none
where the time goes in v2:
time: 50.5 us; the launch traced here: 50.3 us
  Pallas kernels  49.6 us (98%)
  between operations  0.64 us (1%)
    pallas_call x1, Pallas kernels, local(): pl.pallas_call(kernel, out_shape=jax.ShapeDtypeStruct((16, TESTS), f32),...  48.3 us
    pallas_call x1, Pallas kernels, local(): pl.pallas_call(split_result, out_shape=(jax.ShapeDtypeStruct((4, TERMS //...  1.28 us

profile of v2, /device:TPU:1, one launch (start us, length us, event | category | flops | bytes accessed | tf_op | source)
XLA Modules:
  0.0 50.3 jit_solution(13883717785010693062)
XLA Ops:
  0.6 48.3 %weak_form_fit.1.result_ref = f32[16,128]{1,0:T(8,128)} custom-call(s32[7,128]{1,0:T(8,128)} %bitcast.1, f32[7,1]{1,0:T(8,128)} %constant.8.clone.code_weight_ref, f32[1,1632]{1,0:T(1,128)} %constant.9.clone.keys_ref, bf16[4,8,128,256]{3,2,1,0:T(8,128)(2,1)} %start_ref.1, bf16[4,8,128,256]{3,2,1,0:T(8,128)(2,1)} %end_ref.1, ...), custom_call_target="tpu_custom_call" | custom-call | tf_op jit(solution)/shard_map/weak_form_fit/pallas_call | solution.py:528
  49.0 1.3 %split_result.1 = (f32[4,128]{1,0:T(4,128)}, f32[4,128]{1,0:T(4,128)}) custom-call(f32[16,128]{1,0:T(8,128)} %weak_form_fit.1.result_ref), custom_call_target="tpu_custom_call" | custom-call | tf_op jit(solution)/shard_map/split_result/pallas_call | solution.py:575

commit v3 on v2

--- a/solution.py
+++ b/solution.py
@@ -22,6 +22,9 @@
 CELLS_X = 8
 CELLS_Y = 40
 CELLS_XY = CELLS_X * CELLS_Y
+MAIN_Y = 32
+MAIN = CELLS_X * MAIN_Y
+REST = CELLS_XY - MAIN
 WIDTH_Z = 256
 CENTERS_Y = 4
 CENTERS_Z = 32
@@ -84,8 +87,13 @@
                         full[side, center, order_x * 3 + order_y] = tap(
                             order_x, x - STRIDE * side
                         ) * tap(order_y, y - STRIDE * center - shift)
-        high, low = split_pieces(full.reshape(2, CENTERS_Y * PAD, CELLS_XY))
-        both.append(np.concatenate([high, low], axis=1))
+        wide = full[..., :MAIN_Y].reshape(2, CENTERS_Y * PAD, MAIN)
+        edge = full[:, CENTERS_Y - 1, :, :, MAIN_Y:].reshape(2, PAD, REST)
+        apart = np.zeros((2, 4, PAD, 4, REST))
+        for member in range(4):
+            apart[:, member, :, member, :] = edge
+        groups = (wide, apart.reshape(2, 4 * PAD, 4 * REST))
+        both.append(np.stack([np.concatenate(split_pieces(g), axis=1) for g in groups]))
     return np.stack(both)
 
 
@@ -143,21 +151,15 @@
         }
 
 
-def products(fields_ref, later_ref, wide_ref, theta_ref):
+def products(fields_ref, later_ref, wide_ref, theta_ref, rest_ref):
     for field in range(4):
         for x in range(CELLS_X):
-            wide_ref[field, x * CELLS_Y : (x + 1) * CELLS_Y, :] = fields_ref[field, x].astype(f32)
-            wide_ref[4 + field, x * CELLS_Y : (x + 1) * CELLS_Y, :] = later_ref[field, x].astype(
-                f32
-            )
-
-    def rows(step, carry):
-        at = pl.multiple_of(step * 16, 16)
-        for half in range(2):
-            some(at, slice(half * 128, half * 128 + 128))
-        return carry
-
-    def some(at, lanes):
+            for base, source in ((0, fields_ref), (4, later_ref)):
+                plane = source[field, x].astype(f32)
+                wide_ref[base + field, x * MAIN_Y : x * MAIN_Y + MAIN_Y, :] = plane[:MAIN_Y]
+                wide_ref[base + field, MAIN + x * 8 : MAIN + x * 8 + 8, :] = plane[MAIN_Y:]
+
+    def some(at, lanes, put):
         value = [wide_ref[field, pl.ds(at, 16), lanes] for field in range(4)]
         square = [v * v for v in value]
         pairs = {}
@@ -176,55 +178,92 @@
                 else:
                     result = result * factor
                     pairs[key] = result
-            theta_ref[index, pl.ds(at, 16), lanes] = result.astype(bf16)
+            put(index, result.astype(bf16))
         for field in range(4):
             change = wide_ref[4 + field, pl.ds(at, 16), lanes] - value[field]
-            theta_ref[len(POWERS) + field, pl.ds(at, 16), lanes] = change.astype(bf16)
-
-    lax.fori_loop(0, CELLS_XY // 16, rows, 0)
-
-
-def plane_sums(weights_ref, theta_ref, plane_ref, side):
+            put(len(POWERS) + field, change.astype(bf16))
+
+    def main_rows(step, carry):
+        at = pl.multiple_of(step * 16, 16)
+        for half in range(2):
+
+            def put(index, value, half=half):
+                lane = index % 2 * WIDTH_Z + half * 128
+                theta_ref[index // 2, pl.ds(at, 16), lane : lane + 128] = value
+
+            some(at, slice(half * 128, half * 128 + 128), put)
+        return carry
+
+    def rest_rows(step, carry):
+        at = pl.multiple_of(step * 16, 16)
+        for half in range(2):
+            lanes = slice(half * 128, half * 128 + 128)
+
+            def put(index, value, lanes=lanes):
+                rest_ref[index // 4, pl.ds(index % 4 * REST + at, 16), lanes] = value
+
+            some(MAIN + at, lanes, put)
+        return carry
+
+    lax.fori_loop(0, MAIN // 16, main_rows, 0)
+    lax.fori_loop(0, REST // 16, rest_rows, 0)
+    used = PRODUCTS % 4 * REST
+    rest_ref[PRODUCTS // 4, used:, :] = jnp.zeros((4 * REST - used, WIDTH_Z), bf16)
+
+
+def plane_sums(weights_ref, theta_ref, rest_ref, rest_sum_ref, plane_ref, side, pieces):
     half = CENTERS_Y * PAD
 
-    def one(index, carry):
-        both = jnp.dot(weights_ref[side], theta_ref[index], preferred_element_type=f32)
+    def leftover(index, carry):
+        both = jnp.dot(weights_ref[1, side], rest_ref[index], preferred_element_type=f32)
+        at = pl.multiple_of(index * half, half)
+        rest_sum_ref[pl.ds(at, half), :] = both[:half] + both[half:]
+        return carry
+
+    def pair(index, carry):
+        both = jnp.dot(weights_ref[0, side], theta_ref[index], preferred_element_type=f32)
         total = both[:half] + both[half:]
-        high = total.astype(bf16)
-        low = (total - high.astype(f32)).astype(bf16)
-        at = pl.multiple_of(index * PAD, PAD)
-        for center in range(CENTERS_Y):
-            row = center * PAD
-            lanes = slice(center * WIDTH_Z, (center + 1) * WIDTH_Z)
-            plane_ref[side, 0, pl.ds(at, PAD), lanes] = high[row : row + PAD]
-            plane_ref[side, 1, pl.ds(at, PAD), lanes] = low[row : row + PAD]
+        for member in range(2):
+            at = pl.multiple_of((index * 2 + member) * PAD, PAD)
+            for center in range(CENTERS_Y):
+                part = total[center * PAD : center * PAD + PAD, member * WIDTH_Z :][:, :WIDTH_Z]
+                if center == CENTERS_Y - 1:
+                    part = part + rest_sum_ref[pl.ds(at, PAD), :]
+                lanes = slice(center * WIDTH_Z, (center + 1) * WIDTH_Z)
+                high = part.astype(bf16)
+                plane_ref[0, pl.ds(at, PAD), lanes] = high
+                if pieces == 2:
+                    plane_ref[1, pl.ds(at, PAD), lanes] = (part - high.astype(f32)).astype(bf16)
         return carry
 
-    lax.fori_loop(0, PRODUCTS, one, 0, unroll=2)
-
-
-def depth_sums(plane_ref, depth_ref, table_ref, side):
-    size = 2 * PAD * 17 // 2
+    lax.fori_loop(0, PRODUCTS // 4 + 1, leftover, 0, unroll=9)
+    lax.fori_loop(0, PRODUCTS // 2, pair, 0, unroll=PRODUCTS // 2)
+
+
+def depth_sums(plane_ref, depth_ref, table_ref, pieces):
+    size = TABLE // 2
     for start in range(0, TABLE, size):
-        high = jnp.dot(
-            plane_ref[side, 0, start : start + size], depth_ref[...], preferred_element_type=f32
+        total = jnp.dot(
+            plane_ref[0, start : start + size], depth_ref[...], preferred_element_type=f32
         )
-        low = jnp.dot(
-            plane_ref[side, 1, start : start + size], depth_ref[...], preferred_element_type=f32
-        )
-        total = high + low
+        if pieces == 2:
+            total = total + jnp.dot(
+                plane_ref[1, start : start + size], depth_ref[...], preferred_element_type=f32
+            )
         top = total.astype(bf16)
         rest = (total - top.astype(f32)).astype(bf16)
         for order in range(3):
             lanes = slice(order * TESTS, (order + 1) * TESTS)
             rows = slice(order * TABLE + start, order * TABLE + start + size)
             table_ref[rows, :TESTS] = top[:, lanes]
-            table_ref[rows, TESTS:] = rest[:, lanes]
+            if pieces == 2:
+                table_ref[rows, TESTS:] = rest[:, lanes]
 
 
 def pick_table(codes_ref, keys_ref, pick_ref):
+    spread = [jnp.broadcast_to(codes_ref[part, :1, :], (128, 128)).T for part in range(5)]
     for row in range(0, PICKED, 16):
-        code = codes_ref[row // 128, row % 128 : row % 128 + 16, :]
+        code = spread[row // 128][row % 128 : row % 128 + 16, :]
         for column in range(0, KEYS, 128):
             width = min(128, KEYS - column)
             same = code[:, :width] == keys_ref[:, column : column + width]
@@ -315,6 +354,8 @@
     depth_ref,
     wide_ref,
     theta_ref,
+    rest_ref,
+    rest_sum_ref,
     plane_ref,
     table_ref,
     codes_ref,
@@ -372,13 +413,13 @@
     code = jnp.sum(
         exponents_ref[...].astype(f32) * code_weight_ref[...], axis=0, keepdims=True
     )
-    codes_ref[lib] = jnp.broadcast_to(code, (128, 128)).T
-    row = lax.broadcasted_iota(jnp.int32, (16, 128), 0)
-    codes_ref[4, :16, :] = jnp.where(row < 4, TARGET_CODE + row, -1).astype(f32)
+    codes_ref[lib] = jnp.broadcast_to(code, (8, 128))
+    lane = lax.broadcasted_iota(jnp.int32, (8, 128), 1)
+    codes_ref[4] = jnp.where(lane < 4, TARGET_CODE + lane, -1).astype(f32)
 
     loads[0].wait()
     loads[1].wait()
-    products(fields_ref, later_ref, wide_ref, theta_ref)
+    products(fields_ref, later_ref, wide_ref, theta_ref, rest_ref)
     pl.semaphore_wait(barrier, CHIPS - 1 + 5)
     code_copies = [
         pltpu.make_async_remote_copy(
@@ -394,13 +435,13 @@
     for copy in code_copies:
         copy.start()
     loads[2].wait()
-    plane_sums(weights_ref, theta_ref, plane_ref, 1)
+    plane_sums(weights_ref, theta_ref, rest_ref, rest_sum_ref, plane_ref, 1, 2)
+    loads[3].wait()
+    depth_sums(plane_ref, depth_ref, table_ref, 2)
     for copy in code_copies:
         copy.wait()
     pick_table(codes_ref, keys_ref, pick_ref)
-    loads[3].wait()
-    depth_sums(plane_ref, depth_ref, table_ref.at[1], 1)
-    both = jnp.dot(pick_ref[...], table_ref[1], preferred_element_type=f32)
+    both = jnp.dot(pick_ref[...], table_ref[...], preferred_element_type=f32)
     edge_out_ref[...] = (both[:, :TESTS] + both[:, TESTS:]).astype(bf16)
     edge = pltpu.make_async_remote_copy(
         src_ref=edge_out_ref,
@@ -411,18 +452,25 @@
         device_id_type=MESH,
     )
     edge.start()
-    plane_sums(weights_ref, theta_ref, plane_ref, 0)
-    depth_sums(plane_ref, depth_ref, table_ref.at[0], 0)
-    both = jnp.dot(pick_ref[...], table_ref[0], preferred_element_type=f32)
+    plane_sums(weights_ref, theta_ref, rest_ref, rest_sum_ref, plane_ref, 0, 2)
+    depth_sums(plane_ref, depth_ref, table_ref, 2)
+    both = jnp.dot(pick_ref[...], table_ref[...], preferred_element_type=f32)
     lib_ref[...] = both[:, :TESTS] + both[:, TESTS:]
     edge.wait()
     keep = jnp.where(sub > 0, 1.0, 0.0).astype(f32)
     lib_ref[...] = lib_ref[...] + keep * edge_in_ref[...].astype(f32)
 
-    library = lib_ref[:TERMS]
-    gram_ref[...] = whole_dot(library, library, 1)
+    high = lib_ref[...].astype(bf16)
+    low = (lib_ref[...] - high.astype(f32)).astype(bf16)
+    product = lax.dot_general(
+        jnp.concatenate([high, low, high], axis=1),
+        jnp.concatenate([high[:TERMS], high[:TERMS], low[:TERMS]], axis=1),
+        (((1,), (1,)), ((), ())),
+        preferred_element_type=f32,
+    )
+    gram_ref[...] = product[:TERMS]
+    cross = product[TERMS : TERMS + 8]
     target = lib_ref[TERMS : TERMS + 8]
-    cross = whole_dot(target, library, 1)
     squares = jnp.broadcast_to(jnp.sum(target * target, axis=1, keepdims=True), (8, 128))
 
     for piece in range(8):
@@ -533,13 +581,15 @@
         scratch_shapes=[
             pltpu.VMEM((4, CELLS_X, CELLS_Y, WIDTH_Z), bf16),
             pltpu.VMEM((4, CELLS_X, CELLS_Y, WIDTH_Z), bf16),
-            pltpu.VMEM((2, 2 * CENTERS_Y * PAD, CELLS_XY), bf16),
+            pltpu.VMEM((2, 2, 2 * CENTERS_Y * PAD, MAIN), bf16),
             pltpu.VMEM((CENTERS_Y * WIDTH_Z, 3 * TESTS), bf16),
             pltpu.VMEM((8, CELLS_XY, WIDTH_Z), f32),
-            pltpu.VMEM((PRODUCTS, CELLS_XY, WIDTH_Z), bf16),
-            pltpu.VMEM((2, 2, TABLE, CENTERS_Y * WIDTH_Z), bf16),
-            pltpu.VMEM((2, KEYS, 2 * TESTS), bf16),
-            pltpu.VMEM((5, 128, 128), f32),
+            pltpu.VMEM((PRODUCTS // 2, MAIN, 2 * WIDTH_Z), bf16),
+            pltpu.VMEM((PRODUCTS // 4 + 1, 4 * REST, WIDTH_Z), bf16),
+            pltpu.VMEM(((PRODUCTS // 4 + 1) * 4 * PAD, WIDTH_Z), f32),
+            pltpu.VMEM((2, TABLE, CENTERS_Y * WIDTH_Z), bf16),
+            pltpu.VMEM((KEYS, 2 * TESTS), bf16),
+            pltpu.VMEM((5, 8, 128), f32),
             pltpu.VMEM((PICKED, KEYS), bf16),
             pltpu.VMEM((PICKED, TESTS), bf16),
             pltpu.VMEM((PICKED, TESTS), bf16),

time: 50.5 us -> 46.8 us (0.927)
  Pallas kernels: 49.6 us -> 45.9 us
    pallas_call x1, Pallas kernels: 48.3 us -> 44.7 us  [local(): pl.pallas_call(kernel, out_shape=jax.ShapeDtypeStruct((16, TESTS), f32),...]
where the time goes in v3:
time: 46.8 us; the launch traced here: 46.6 us
  Pallas kernels  45.9 us (98%)
  between operations  0.64 us (1%)
    pallas_call x1, Pallas kernels, local(): pl.pallas_call(kernel, out_shape=jax.ShapeDtypeStruct((16, TESTS), f32),...  44.7 us
    pallas_call x1, Pallas kernels, local(): pl.pallas_call(split_result, out_shape=(jax.ShapeDtypeStruct((4, TERMS //...  1.28 us

profile of v3, /device:TPU:1, one launch (start us, length us, event | category | flops | bytes accessed | tf_op | source)
XLA Modules:
  0.0 46.6 jit_solution(17225151699208201967)
XLA Ops:
  0.6 44.7 %weak_form_fit.1.result_ref = f32[16,128]{1,0:T(8,128)} custom-call(s32[7,128]{1,0:T(8,128)} %bitcast.1, f32[7,1]{1,0:T(8,128)} %constant.8.clone.code_weight_ref, f32[1,1632]{1,0:T(1,128)} %constant.9.clone.keys_ref, bf16[4,8,128,256]{3,2,1,0:T(8,128)(2,1)} %start_ref.1, bf16[4,8,128,256]{3,2,1,0:T(8,128)(2,1)} %end_ref.1, ...), custom_call_target="tpu_custom_call" | custom-call | tf_op jit(solution)/shard_map/weak_form_fit/pallas_call | solution.py:576
  45.3 1.3 %split_result.1 = (f32[4,128]{1,0:T(4,128)}, f32[4,128]{1,0:T(4,128)}) custom-call(f32[16,128]{1,0:T(8,128)} %weak_form_fit.1.result_ref), custom_call_target="tpu_custom_call" | custom-call | tf_op jit(solution)/shard_map/split_result/pallas_call | solution.py:625

commit v4 on v3

--- a/solution.py
+++ b/solution.py
@@ -302,6 +302,7 @@
             block = gram_ref[rows, lanes] * (inverse_column[i] / total) * inverse_row[j]
             if i == j:
                 block = block + jnp.where(same, RIDGE, 0.0)
+            gram_ref[rows, lanes] = block
             high = block.astype(bf16)
             normal_ref[rows, lanes] = high
             normal_ref[rows, slice(TERMS + j * 128, TERMS + j * 128 + 128)] = (
@@ -318,12 +319,33 @@
         both = jnp.dot(stacked, normal_ref[...], preferred_element_type=f32)
         return both[:8, :TERMS] + both[:8, TERMS:] + both[8:, :TERMS]
 
-    vector = jnp.full((8, TERMS), TERMS**-0.5, f32)
-    for _ in range(POWER - 1):
-        vector = apply(vector)
-    applied = apply(vector)
-    before = jnp.sum(vector * vector, axis=1, keepdims=True)
-    after = jnp.sum(applied * applied, axis=1, keepdims=True)
+    def fold(column):
+        sums = [jnp.zeros((8, TERMS), f32) for _ in range(4)]
+        for tile in range(TERMS // 8):
+            rows = gram_ref[tile * 8 : tile * 8 + 8, :]
+            if column is not None:
+                rows = rows * column[tile]
+            sums[tile % 4] = sums[tile % 4] + rows
+        return jnp.sum((sums[0] + sums[1]) + (sums[2] + sums[3]), axis=0, keepdims=True)
+
+    def spread(row):
+        row = jnp.broadcast_to(row, (8, TERMS))
+        return [
+            jnp.sum(gram_ref[tile * 8 : tile * 8 + 8, :] * row, axis=1, keepdims=True)
+            for tile in range(TERMS // 8)
+        ]
+
+    column = None
+    for sweep in range(POWER // 2):
+        row = fold(column)
+        if sweep == 0:
+            row = row * TERMS**-0.5
+        column = spread(row)
+    before = jnp.sum(row * row, axis=1, keepdims=True)
+    after = column[0] * column[0]
+    for tile in range(1, TERMS // 8):
+        after = after + column[tile] * column[tile]
+    after = jnp.sum(after, axis=0, keepdims=True)
     step_size = jnp.sqrt(before) / jnp.sqrt(after)
     bound = step_size * SHRINK
     coeffs = None
@@ -377,6 +399,7 @@
     part_sems,
     done_sems,
     other_sems,
+    ready_sems,
 ):
     sub = lax.axis_index("sub")
     lib = lax.axis_index("lib")
@@ -399,15 +422,10 @@
 
     barrier = pltpu.get_barrier_semaphore()
 
-    for d in PARTNERS:
-        pl.semaphore_signal(barrier, inc=1, device_id=chips.device(d), device_id_type=MESH)
-    for device in (
-        next_sub,
-        last_sub,
-        {"sub": sub, "lib": (lib + 1) % 4},
-        {"sub": sub, "lib": (lib + 2) % 4},
-        {"sub": sub, "lib": (lib + 3) % 4},
-    ):
+    near = [chips.device(d) for d in (1, 2, 3, 4, 8, 12, 16, 32, 48)]
+    near += [{"sub": sub, "lib": (lib + step) % 4} for step in (1, 2, 3)]
+    near += [next_sub, last_sub]
+    for device in near:
         pl.semaphore_signal(barrier, inc=1, device_id=device, device_id_type=MESH)
 
     code = jnp.sum(
@@ -420,7 +438,9 @@
     loads[0].wait()
     loads[1].wait()
     products(fields_ref, later_ref, wide_ref, theta_ref, rest_ref)
-    pl.semaphore_wait(barrier, CHIPS - 1 + 5)
+    pl.semaphore_wait(barrier, len(near))
+    for device in near[6:9]:
+        pl.semaphore_signal(ready_sems.at[0], inc=1, device_id=device, device_id_type=MESH)
     code_copies = [
         pltpu.make_async_remote_copy(
             src_ref=codes_ref.at[lib],
@@ -436,6 +456,9 @@
         copy.start()
     loads[2].wait()
     plane_sums(weights_ref, theta_ref, rest_ref, rest_sum_ref, plane_ref, 1, 2)
+    pl.semaphore_wait(ready_sems.at[0], 3)
+    for device in near[3:6]:
+        pl.semaphore_signal(ready_sems.at[1], inc=1, device_id=device, device_id_type=MESH)
     loads[3].wait()
     depth_sums(plane_ref, depth_ref, table_ref, 2)
     for copy in code_copies:
@@ -498,6 +521,7 @@
     pair.start()
     pair.wait()
     half_in_ref[...] = half_in_ref[...] + half_ref[core]
+    pl.semaphore_wait(ready_sems.at[1], 3)
     own = chips.chip(0)
     for d in PARTNERS:
         pltpu.make_async_remote_copy(
@@ -608,6 +632,7 @@
             pltpu.SemaphoreType.DMA((2,)),
             pltpu.SemaphoreType.DMA((2,)),
             pltpu.SemaphoreType.DMA((2,)),
+            pltpu.SemaphoreType.REGULAR((2,)),
         ],
         compiler_params=pltpu.CompilerParams(
             collective_id=0, has_side_effects=True, vmem_limit_bytes=56 << 20

time: 46.8 us -> 45.7 us (0.976)
  Pallas kernels: 45.9 us -> 44.8 us
    pallas_call x1, Pallas kernels: 44.7 us -> 43.6 us  [local(): pl.pallas_call(kernel, out_shape=jax.ShapeDtypeStruct((16, TESTS), f32),...]
where the time goes in v4:
time: 45.7 us; the launch traced here: 45.5 us
  Pallas kernels  44.8 us (98%)
  between operations  0.64 us (1%)
    pallas_call x1, Pallas kernels, local(): pl.pallas_call(kernel, out_shape=jax.ShapeDtypeStruct((16, TESTS), f32),...  43.6 us
    pallas_call x1, Pallas kernels, local(): pl.pallas_call(split_result, out_shape=(jax.ShapeDtypeStruct((4, TERMS //...  1.28 us

profile of v4, /device:TPU:1, one launch (start us, length us, event | category | flops | bytes accessed | tf_op | source)
XLA Modules:
  0.0 45.5 jit_solution(4159323944057579773)
XLA Ops:
  0.6 43.6 %weak_form_fit.1.result_ref = f32[16,128]{1,0:T(8,128)} custom-call(s32[7,128]{1,0:T(8,128)} %bitcast.1, f32[7,1]{1,0:T(8,128)} %constant.8.clone.code_weight_ref, f32[1,1632]{1,0:T(1,128)} %constant.9.clone.keys_ref, bf16[4,8,128,256]{3,2,1,0:T(8,128)(2,1)} %start_ref.1, bf16[4,8,128,256]{3,2,1,0:T(8,128)(2,1)} %end_ref.1, ...), custom_call_target="tpu_custom_call" | custom-call | tf_op jit(solution)/shard_map/weak_form_fit/pallas_call | solution.py:600
  44.2 1.3 %split_result.1 = (f32[4,128]{1,0:T(4,128)}, f32[4,128]{1,0:T(4,128)}) custom-call(f32[16,128]{1,0:T(8,128)} %weak_form_fit.1.result_ref), custom_call_target="tpu_custom_call" | custom-call | tf_op jit(solution)/shard_map/split_result/pallas_call | solution.py:650

commit v5 on v4

--- a/solution.py
+++ b/solution.py
@@ -118,10 +118,6 @@
     for field in range(4):
         codes[0, len(POWERS) + field, 0] = TARGET_CODE + field
     return codes.reshape(1, KEYS)
-
-
-def code_weights():
-    return np.array([[729], [243], [81], [27], [9], [3], [1]], np.float32)
 
 
 def others(value):
@@ -260,16 +256,15 @@
                 table_ref[rows, TESTS:] = rest[:, lanes]
 
 
-def pick_table(codes_ref, keys_ref, pick_ref):
-    spread = [jnp.broadcast_to(codes_ref[part, :1, :], (128, 128)).T for part in range(5)]
-    for row in range(0, PICKED, 16):
-        code = spread[row // 128][row % 128 : row % 128 + 16, :]
+def pick_rows(code, keys_ref, pick_ref, start, count):
+    spread = jnp.broadcast_to(code, (128, 128)).T
+    for row in range(0, count, 16):
         for column in range(0, KEYS, 128):
             width = min(128, KEYS - column)
-            same = code[:, :width] == keys_ref[:, column : column + width]
-            pick_ref[row : row + 16, column : column + width] = jnp.where(same, 1.0, 0.0).astype(
-                bf16
-            )
+            same = spread[row : row + 16, :width] == keys_ref[:, column : column + width]
+            pick_ref[pl.ds(start + row, 16), column : column + width] = jnp.where(
+                same, 1.0, 0.0
+            ).astype(bf16)
 
 
 def whole_dot(left, right, contract):
@@ -362,14 +357,15 @@
 
 
 def kernel(
-    exponents_ref,
-    code_weight_ref,
-    keys_ref,
+    exponents_hbm_ref,
+    keys_hbm_ref,
     start_ref,
     end_ref,
     plane_weight_ref,
     depth_weight_ref,
     result_ref,
+    exponents_ref,
+    keys_ref,
     fields_ref,
     later_ref,
     weights_ref,
@@ -409,16 +405,20 @@
     last_sub = {"sub": (sub + 31) % 32, "lib": lib}
     other_core = {"sub": sub, "lib": lib + 1 - 2 * core}
     window = pl.ds(pl.multiple_of(jnp.maximum(lib * 32 - 8, 0), 8), CELLS_Y)
-    loads = [
-        pltpu.make_async_copy(start_ref.at[:, :, window, :], fields_ref, local_sems.at[0]),
-        pltpu.make_async_copy(end_ref.at[:, :, window, :], later_ref, local_sems.at[1]),
-        pltpu.make_async_copy(
-            plane_weight_ref.at[jnp.minimum(lib, 1)], weights_ref, local_sems.at[2]
-        ),
-        pltpu.make_async_copy(depth_weight_ref, depth_ref, local_sems.at[3]),
-    ]
-    for load in loads:
-        load.start()
+    load_exponents = pltpu.make_async_copy(exponents_hbm_ref, exponents_ref, local_sems.at[4])
+    load_exponents.start()
+    for field in range(4):
+        for number, (source, target) in enumerate(
+            ((start_ref, fields_ref), (end_ref, later_ref))
+        ):
+            pltpu.make_async_copy(
+                source.at[field, :, window, :], target.at[field], local_sems.at[number]
+            ).start()
+    load_weights = pltpu.make_async_copy(
+        plane_weight_ref.at[jnp.minimum(lib, 1)], weights_ref, local_sems.at[2]
+    )
+    load_depth = pltpu.make_async_copy(depth_weight_ref, depth_ref, local_sems.at[3])
+    load_keys = pltpu.make_async_copy(keys_hbm_ref, keys_ref, local_sems.at[5])
 
     barrier = pltpu.get_barrier_semaphore()
 
@@ -428,15 +428,19 @@
     for device in near:
         pl.semaphore_signal(barrier, inc=1, device_id=device, device_id_type=MESH)
 
-    code = jnp.sum(
-        exponents_ref[...].astype(f32) * code_weight_ref[...], axis=0, keepdims=True
-    )
+    load_weights.start()
+    load_depth.start()
+    load_keys.start()
+    load_exponents.wait()
+    code = jnp.zeros((1, 128), f32)
+    for place in range(7):
+        code = code * 3.0 + exponents_ref[place : place + 1, :].astype(f32)
     codes_ref[lib] = jnp.broadcast_to(code, (8, 128))
     lane = lax.broadcasted_iota(jnp.int32, (8, 128), 1)
     codes_ref[4] = jnp.where(lane < 4, TARGET_CODE + lane, -1).astype(f32)
 
-    loads[0].wait()
-    loads[1].wait()
+    pltpu.make_async_copy(fields_ref, fields_ref, local_sems.at[0]).wait()
+    pltpu.make_async_copy(later_ref, later_ref, local_sems.at[1]).wait()
     products(fields_ref, later_ref, wide_ref, theta_ref, rest_ref)
     pl.semaphore_wait(barrier, len(near))
     for device in near[6:9]:
@@ -454,32 +458,44 @@
     ]
     for copy in code_copies:
         copy.start()
-    loads[2].wait()
+    load_weights.wait()
     plane_sums(weights_ref, theta_ref, rest_ref, rest_sum_ref, plane_ref, 1, 2)
     pl.semaphore_wait(ready_sems.at[0], 3)
     for device in near[3:6]:
         pl.semaphore_signal(ready_sems.at[1], inc=1, device_id=device, device_id_type=MESH)
-    loads[3].wait()
+    load_depth.wait()
+    load_keys.wait()
     depth_sums(plane_ref, depth_ref, table_ref, 2)
-    for copy in code_copies:
+    edges = []
+
+    def send_edge(number, code_row, start, count):
+        rows = pl.ds(start, count)
+        pick_rows(code_row, keys_ref, pick_ref, start, count)
+        both = jnp.dot(pick_ref[rows, :], table_ref[...], preferred_element_type=f32)
+        edge_out_ref[rows, :] = (both[:, :TESTS] + both[:, TESTS:]).astype(bf16)
+        edge = pltpu.make_async_remote_copy(
+            src_ref=edge_out_ref.at[rows],
+            dst_ref=edge_in_ref.at[rows],
+            send_sem=edge_sems.at[number],
+            recv_sem=edge_sems.at[5 + number],
+            device_id=next_sub,
+            device_id_type=MESH,
+        )
+        edge.start()
+        edges.append(edge)
+
+    send_edge(0, code, pl.multiple_of(lib * 128, 128), 128)
+    send_edge(1, codes_ref[4, :1, :], TERMS, 16)
+    for step, copy in enumerate(code_copies):
         copy.wait()
-    pick_table(codes_ref, keys_ref, pick_ref)
-    both = jnp.dot(pick_ref[...], table_ref[...], preferred_element_type=f32)
-    edge_out_ref[...] = (both[:, :TESTS] + both[:, TESTS:]).astype(bf16)
-    edge = pltpu.make_async_remote_copy(
-        src_ref=edge_out_ref,
-        dst_ref=edge_in_ref,
-        send_sem=edge_sems.at[0],
-        recv_sem=edge_sems.at[1],
-        device_id=next_sub,
-        device_id_type=MESH,
-    )
-    edge.start()
+        part = (lib + 3 - step) % 4
+        send_edge(2 + step, codes_ref[part, :1, :], pl.multiple_of(part * 128, 128), 128)
     plane_sums(weights_ref, theta_ref, rest_ref, rest_sum_ref, plane_ref, 0, 2)
     depth_sums(plane_ref, depth_ref, table_ref, 2)
     both = jnp.dot(pick_ref[...], table_ref[...], preferred_element_type=f32)
     lib_ref[...] = both[:, :TESTS] + both[:, TESTS:]
-    edge.wait()
+    for edge in edges:
+        edge.wait()
     keep = jnp.where(sub > 0, 1.0, 0.0).astype(f32)
     lib_ref[...] = lib_ref[...] + keep * edge_in_ref[...].astype(f32)
 
@@ -600,9 +616,11 @@
     result = pl.pallas_call(
         kernel,
         out_shape=jax.ShapeDtypeStruct((16, TESTS), f32),
-        in_specs=[vmem, vmem, vmem, anywhere, anywhere, anywhere, anywhere],
+        in_specs=[anywhere] * 6,
         out_specs=vmem,
         scratch_shapes=[
+            pltpu.VMEM((7, 128), jnp.int32),
+            pltpu.VMEM((1, KEYS), f32),
             pltpu.VMEM((4, CELLS_X, CELLS_Y, WIDTH_Z), bf16),
             pltpu.VMEM((4, CELLS_X, CELLS_Y, WIDTH_Z), bf16),
             pltpu.VMEM((2, 2, 2 * CENTERS_Y * PAD, MAIN), bf16),
@@ -625,9 +643,9 @@
             pltpu.VMEM((2, CHIPS, CHUNK, 128), f32),
             pltpu.VMEM((TERMS, 2 * TERMS), bf16),
             pltpu.VMEM((8, TERMS), f32),
-            pltpu.SemaphoreType.DMA((4,)),
             pltpu.SemaphoreType.DMA((6,)),
-            pltpu.SemaphoreType.DMA((2,)),
+            pltpu.SemaphoreType.DMA((6,)),
+            pltpu.SemaphoreType.DMA((10,)),
             pltpu.SemaphoreType.DMA((2,)),
             pltpu.SemaphoreType.DMA((2,)),
             pltpu.SemaphoreType.DMA((2,)),
@@ -640,7 +658,6 @@
         name="weak_form_fit",
     )(
         exponents.T,
-        jnp.asarray(code_weights()),
         jnp.asarray(column_codes()),
         snap_start,
         snap_end,

time: 45.7 us -> 44.5 us (0.974)
  Pallas kernels: 44.8 us -> 43.6 us
    pallas_call x1, Pallas kernels: 43.6 us -> 42.4 us  [local(): pl.pallas_call(kernel, out_shape=jax.ShapeDtypeStruct((16, TESTS), f32),...]
where the time goes in v5:
time: 44.5 us; the launch traced here: 44.3 us
  Pallas kernels  43.6 us (98%)
  between operations  0.64 us (1%)
    pallas_call x1, Pallas kernels, local(): pl.pallas_call(kernel, out_shape=jax.ShapeDtypeStruct((16, TESTS), f32),...  42.4 us
    pallas_call x1, Pallas kernels, local(): pl.pallas_call(split_result, out_shape=(jax.ShapeDtypeStruct((4, TERMS //...  1.28 us

profile of v5, /device:TPU:1, one launch (start us, length us, event | category | flops | bytes accessed | tf_op | source)
XLA Modules:
  0.0 44.3 jit_solution(17857609317800453158)
XLA Ops:
  0.6 42.4 %weak_form_fit.1.result_ref = f32[16,128]{1,0:T(8,128)} custom-call(s32[7,128]{1,0:T(8,128)} %bitcast.1, f32[1,1632]{1,0:T(1,128)} %constant.6.clone.keys_hbm_ref, bf16[4,8,128,256]{3,2,1,0:T(8,128)(2,1)} %start_ref.1, bf16[4,8,128,256]{3,2,1,0:T(8,128)(2,1)} %end_ref.1, bf16[2,2,2,128,256]{4,3,2,1,0:T(8,128)(2,1)} %constant.7.clone.plane_weight_ref, ...), custom_call_target="tpu_custom_call" | custom-call | tf_op jit(solution)/shard_map/weak_form_fit/pallas_call | solution.py:616
  43.0 1.3 %split_result.1 = (f32[4,128]{1,0:T(4,128)}, f32[4,128]{1,0:T(4,128)}) custom-call(f32[16,128]{1,0:T(8,128)} %weak_form_fit.1.result_ref), custom_call_target="tpu_custom_call" | custom-call | tf_op jit(solution)/shard_map/split_result/pallas_call | solution.py:667

commit v6 on v5

--- a/solution.py
+++ b/solution.py
@@ -207,7 +207,7 @@
     rest_ref[PRODUCTS // 4, used:, :] = jnp.zeros((4 * REST - used, WIDTH_Z), bf16)
 
 
-def plane_sums(weights_ref, theta_ref, rest_ref, rest_sum_ref, plane_ref, side, pieces):
+def plane_sums(weights_ref, theta_ref, rest_ref, rest_sum_ref, plane_ref, side):
     half = CENTERS_Y * PAD
 
     def leftover(index, carry):
@@ -228,31 +228,29 @@
                 lanes = slice(center * WIDTH_Z, (center + 1) * WIDTH_Z)
                 high = part.astype(bf16)
                 plane_ref[0, pl.ds(at, PAD), lanes] = high
-                if pieces == 2:
-                    plane_ref[1, pl.ds(at, PAD), lanes] = (part - high.astype(f32)).astype(bf16)
+                plane_ref[1, pl.ds(at, PAD), lanes] = (part - high.astype(f32)).astype(bf16)
         return carry
 
     lax.fori_loop(0, PRODUCTS // 4 + 1, leftover, 0, unroll=9)
     lax.fori_loop(0, PRODUCTS // 2, pair, 0, unroll=PRODUCTS // 2)
 
 
-def depth_sums(plane_ref, depth_ref, table_ref, pieces):
+def depth_sums(plane_ref, depth_ref, table_ref, keep_low):
     size = TABLE // 2
     for start in range(0, TABLE, size):
         total = jnp.dot(
             plane_ref[0, start : start + size], depth_ref[...], preferred_element_type=f32
         )
-        if pieces == 2:
-            total = total + jnp.dot(
-                plane_ref[1, start : start + size], depth_ref[...], preferred_element_type=f32
-            )
+        total = total + jnp.dot(
+            plane_ref[1, start : start + size], depth_ref[...], preferred_element_type=f32
+        )
         top = total.astype(bf16)
         rest = (total - top.astype(f32)).astype(bf16)
         for order in range(3):
             lanes = slice(order * TESTS, (order + 1) * TESTS)
             rows = slice(order * TABLE + start, order * TABLE + start + size)
             table_ref[rows, :TESTS] = top[:, lanes]
-            if pieces == 2:
+            if keep_low:
                 table_ref[rows, TESTS:] = rest[:, lanes]
 
 
@@ -424,9 +422,18 @@
 
     near = [chips.device(d) for d in (1, 2, 3, 4, 8, 12, 16, 32, 48)]
     near += [{"sub": sub, "lib": (lib + step) % 4} for step in (1, 2, 3)]
-    near += [next_sub, last_sub]
     for device in near:
         pl.semaphore_signal(barrier, inc=1, device_id=device, device_id_type=MESH)
+    sends = sub < 31
+    receives = sub > 0
+
+    @pl.when(sends)
+    def _():
+        pl.semaphore_signal(barrier, inc=1, device_id=next_sub, device_id_type=MESH)
+
+    @pl.when(receives)
+    def _():
+        pl.semaphore_signal(barrier, inc=1, device_id=last_sub, device_id_type=MESH)
 
     load_weights.start()
     load_depth.start()
@@ -442,7 +449,7 @@
     pltpu.make_async_copy(fields_ref, fields_ref, local_sems.at[0]).wait()
     pltpu.make_async_copy(later_ref, later_ref, local_sems.at[1]).wait()
     products(fields_ref, later_ref, wide_ref, theta_ref, rest_ref)
-    pl.semaphore_wait(barrier, len(near))
+    pl.semaphore_wait(barrier, len(near) + jnp.minimum(sub, 1) + jnp.minimum(31 - sub, 1))
     for device in near[6:9]:
         pl.semaphore_signal(ready_sems.at[0], inc=1, device_id=device, device_id_type=MESH)
     code_copies = [
@@ -459,20 +466,21 @@
     for copy in code_copies:
         copy.start()
     load_weights.wait()
-    plane_sums(weights_ref, theta_ref, rest_ref, rest_sum_ref, plane_ref, 1, 2)
+    plane_sums(weights_ref, theta_ref, rest_ref, rest_sum_ref, plane_ref, 1)
     pl.semaphore_wait(ready_sems.at[0], 3)
     for device in near[3:6]:
         pl.semaphore_signal(ready_sems.at[1], inc=1, device_id=device, device_id_type=MESH)
     load_depth.wait()
     load_keys.wait()
-    depth_sums(plane_ref, depth_ref, table_ref, 2)
+    depth_sums(plane_ref, depth_ref, table_ref, False)
     edges = []
 
     def send_edge(number, code_row, start, count):
         rows = pl.ds(start, count)
         pick_rows(code_row, keys_ref, pick_ref, start, count)
-        both = jnp.dot(pick_ref[rows, :], table_ref[...], preferred_element_type=f32)
-        edge_out_ref[rows, :] = (both[:, :TESTS] + both[:, TESTS:]).astype(bf16)
+        edge_out_ref[rows, :] = jnp.dot(
+            pick_ref[rows, :], table_ref[:, :TESTS], preferred_element_type=f32
+        ).astype(bf16)
         edge = pltpu.make_async_remote_copy(
             src_ref=edge_out_ref.at[rows],
             dst_ref=edge_in_ref.at[rows],
@@ -481,8 +489,11 @@
             device_id=next_sub,
             device_id_type=MESH,
         )
-        edge.start()
         edges.append(edge)
+
+        @pl.when(sends)
+        def _():
+            edge.start()
 
     send_edge(0, code, pl.multiple_of(lib * 128, 128), 128)
     send_edge(1, codes_ref[4, :1, :], TERMS, 16)
@@ -490,14 +501,20 @@
         copy.wait()
         part = (lib + 3 - step) % 4
         send_edge(2 + step, codes_ref[part, :1, :], pl.multiple_of(part * 128, 128), 128)
-    plane_sums(weights_ref, theta_ref, rest_ref, rest_sum_ref, plane_ref, 0, 2)
-    depth_sums(plane_ref, depth_ref, table_ref, 2)
+    plane_sums(weights_ref, theta_ref, rest_ref, rest_sum_ref, plane_ref, 0)
+    depth_sums(plane_ref, depth_ref, table_ref, True)
     both = jnp.dot(pick_ref[...], table_ref[...], preferred_element_type=f32)
     lib_ref[...] = both[:, :TESTS] + both[:, TESTS:]
-    for edge in edges:
-        edge.wait()
-    keep = jnp.where(sub > 0, 1.0, 0.0).astype(f32)
-    lib_ref[...] = lib_ref[...] + keep * edge_in_ref[...].astype(f32)
+    @pl.when(sends)
+    def _():
+        for edge in edges:
+            edge.wait_send()
+
+    @pl.when(receives)
+    def _():
+        for edge in edges:
+            edge.wait_recv()
+        lib_ref[...] = lib_ref[...] + edge_in_ref[...].astype(f32)
 
     high = lib_ref[...].astype(bf16)
     low = (lib_ref[...] - high.astype(f32)).astype(bf16)
@@ -507,35 +524,42 @@
         (((1,), (1,)), ((), ())),
         preferred_element_type=f32,
     )
-    gram_ref[...] = product[:TERMS]
     cross = product[TERMS : TERMS + 8]
     target = lib_ref[TERMS : TERMS + 8]
-    squares = jnp.broadcast_to(jnp.sum(target * target, axis=1, keepdims=True), (8, 128))
-
-    for piece in range(8):
-        gram_ref[64 + piece * 4 : 68 + piece * 4, :64] = cross[:4, piece * 64 : piece * 64 + 64]
-    gram_ref[96:100, :64] = squares[:4, :64]
-
-    for half in range(2):
-        for number, (i, j) in enumerate(BLOCKS[half][:4]):
-            lanes = slice(j * 128, j * 128 + 128)
-            for part in range(16):
-                row = i * 128 + part * 8
-                half_ref[half, number * 16 + part, :8, :] = gram_ref[row : row + 8, lanes]
-        i, j = BLOCKS[half][4]
-        for part in range(CHIPS):
-            row = i * 128 + part * 2
-            half_ref[half, part, 8:, :] = gram_ref[row : row + 2, j * 128 : j * 128 + 128]
-    pair = pltpu.make_async_remote_copy(
-        src_ref=half_ref.at[1 - core],
-        dst_ref=half_in_ref,
-        send_sem=core_sems.at[0],
-        recv_sem=core_sems.at[1],
-        device_id=other_core,
-        device_id_type=MESH,
-    )
-    pair.start()
-    pair.wait()
+    squares = jnp.sum(target * target, axis=1, keepdims=True)
+    pairs = []
+    for group in range(2):
+        first = group * CHIPS // 2
+        for half in range(2):
+            for number in range(group * 2, group * 2 + 2):
+                i, j = BLOCKS[half][number]
+                lanes = slice(j * 128, j * 128 + 128)
+                for part in range(16):
+                    row = i * 128 + part * 8
+                    half_ref[half, number * 16 + part, :8, :] = product[row : row + 8, lanes]
+            i, j = BLOCKS[half][4]
+            for part in range(first, first + CHIPS // 2):
+                row = i * 128 + part * 2
+                half_ref[half, part, 8:, :] = product[row : row + 2, j * 128 : j * 128 + 128]
+        if group == 0:
+            for piece in range(8):
+                half_ref[0, 8 + piece // 2, piece % 2 * 4 : piece % 2 * 4 + 4, :64] = cross[
+                    :4, piece * 64 : piece * 64 + 64
+                ]
+            half_ref[0, 12, :4, :64] = jnp.broadcast_to(squares[:4], (4, 64))
+        chunks = pl.ds(first, CHIPS // 2)
+        pair = pltpu.make_async_remote_copy(
+            src_ref=half_ref.at[1 - core, chunks],
+            dst_ref=half_in_ref.at[chunks],
+            send_sem=core_sems.at[group],
+            recv_sem=core_sems.at[2 + group],
+            device_id=other_core,
+            device_id_type=MESH,
+        )
+        pair.start()
+        pairs.append(pair)
+    for pair in pairs:
+        pair.wait()
     half_in_ref[...] = half_in_ref[...] + half_ref[core]
     pl.semaphore_wait(ready_sems.at[1], 3)
     own = chips.chip(0)
@@ -646,7 +670,7 @@
             pltpu.SemaphoreType.DMA((6,)),
             pltpu.SemaphoreType.DMA((6,)),
             pltpu.SemaphoreType.DMA((10,)),
-            pltpu.SemaphoreType.DMA((2,)),
+            pltpu.SemaphoreType.DMA((4,)),
             pltpu.SemaphoreType.DMA((2,)),
             pltpu.SemaphoreType.DMA((2,)),
             pltpu.SemaphoreType.DMA((2,)),

time: 44.5 us -> 43.7 us (0.982)
  Pallas kernels: 43.6 us -> 42.9 us
    pallas_call x1, Pallas kernels: 42.4 us -> 41.6 us  [local(): pl.pallas_call(kernel, out_shape=jax.ShapeDtypeStruct((16, TESTS), f32),...]
where the time goes in v6:
time: 43.7 us; the launch traced here: 43.5 us
  Pallas kernels  42.9 us (98%)
  between operations  0.64 us (1%)
    pallas_call x1, Pallas kernels, local(): pl.pallas_call(kernel, out_shape=jax.ShapeDtypeStruct((16, TESTS), f32),...  41.6 us
    pallas_call x1, Pallas kernels, local(): pl.pallas_call(split_result, out_shape=(jax.ShapeDtypeStruct((4, TERMS //...  1.28 us

profile of v6, /device:TPU:1, one launch (start us, length us, event | category | flops | bytes accessed | tf_op | source)
XLA Modules:
  0.0 43.5 jit_solution(6255040388439600153)
XLA Ops:
  0.6 41.6 %weak_form_fit.1.result_ref = f32[16,128]{1,0:T(8,128)} custom-call(s32[7,128]{1,0:T(8,128)} %bitcast.1, f32[1,1632]{1,0:T(1,128)} %constant.6.clone.keys_hbm_ref, bf16[4,8,128,256]{3,2,1,0:T(8,128)(2,1)} %start_ref.1, bf16[4,8,128,256]{3,2,1,0:T(8,128)(2,1)} %end_ref.1, bf16[2,2,2,128,256]{4,3,2,1,0:T(8,128)(2,1)} %constant.7.clone.plane_weight_ref, ...), custom_call_target="tpu_custom_call" | custom-call | tf_op jit(solution)/shard_map/weak_form_fit/pallas_call | solution.py:640
  42.2 1.3 %split_result.1 = (f32[4,128]{1,0:T(4,128)}, f32[4,128]{1,0:T(4,128)}) custom-call(f32[16,128]{1,0:T(8,128)} %weak_form_fit.1.result_ref), custom_call_target="tpu_custom_call" | custom-call | tf_op jit(solution)/shard_map/split_result/pallas_call | solution.py:691

commit v7 on v6

--- a/solution.py
+++ b/solution.py
@@ -147,16 +147,23 @@
         }
 
 
-def products(fields_ref, later_ref, wide_ref, theta_ref, rest_ref):
+def widen(source_ref, wide_ref, base):
     for field in range(4):
         for x in range(CELLS_X):
-            for base, source in ((0, fields_ref), (4, later_ref)):
-                plane = source[field, x].astype(f32)
-                wide_ref[base + field, x * MAIN_Y : x * MAIN_Y + MAIN_Y, :] = plane[:MAIN_Y]
-                wide_ref[base + field, MAIN + x * 8 : MAIN + x * 8 + 8, :] = plane[MAIN_Y:]
+            plane = source_ref[field, x].astype(f32)
+            wide_ref[base + field, x * MAIN_Y : x * MAIN_Y + MAIN_Y, :] = plane[:MAIN_Y]
+            wide_ref[base + field, MAIN + x * 8 : MAIN + x * 8 + 8, :] = plane[MAIN_Y:]
+
+
+def products(wide_ref, theta_ref, rest_ref, changes):
 
     def some(at, lanes, put):
         value = [wide_ref[field, pl.ds(at, 16), lanes] for field in range(4)]
+        if changes:
+            for field in range(4):
+                change = wide_ref[4 + field, pl.ds(at, 16), lanes] - value[field]
+                put(len(POWERS) + field, change.astype(bf16))
+            return
         square = [v * v for v in value]
         pairs = {}
         for index, powers in enumerate(POWERS):
@@ -175,9 +182,6 @@
                     result = result * factor
                     pairs[key] = result
             put(index, result.astype(bf16))
-        for field in range(4):
-            change = wide_ref[4 + field, pl.ds(at, 16), lanes] - value[field]
-            put(len(POWERS) + field, change.astype(bf16))
 
     def main_rows(step, carry):
         at = pl.multiple_of(step * 16, 16)
@@ -366,6 +370,8 @@
     keys_ref,
     fields_ref,
     later_ref,
+    own_fields_ref,
+    own_later_ref,
     weights_ref,
     depth_ref,
     wide_ref,
@@ -399,21 +405,29 @@
     lib = lax.axis_index("lib")
     chips = Chips()
     core = chips.core
-    next_sub = {"sub": (sub + 1) % 32, "lib": lib}
-    last_sub = {"sub": (sub + 31) % 32, "lib": lib}
+    z = chips.z[0]
+    edge_lib = (lib + 2 * ((z + 1) // 4)) % 4
+    next_sub = {"sub": (sub + 1) % 32, "lib": edge_lib}
+    last_sub = {"sub": (sub + 31) % 32, "lib": (lib + 2 * ((4 - z) // 4)) % 4}
     other_core = {"sub": sub, "lib": lib + 1 - 2 * core}
-    window = pl.ds(pl.multiple_of(jnp.maximum(lib * 32 - 8, 0), 8), CELLS_Y)
+    def load(source_ref, target_ref, part, sem):
+        rows = pl.ds(pl.multiple_of(jnp.maximum(part * 32 - 8, 0), 8), CELLS_Y)
+        for field in range(4):
+            pltpu.make_async_copy(
+                source_ref.at[field, :, rows, :], target_ref.at[field], local_sems.at[sem]
+            ).start()
+
+    def loaded(target_ref, sem):
+        pltpu.make_async_copy(target_ref, target_ref, local_sems.at[sem]).wait()
+
     load_exponents = pltpu.make_async_copy(exponents_hbm_ref, exponents_ref, local_sems.at[4])
     load_exponents.start()
-    for field in range(4):
-        for number, (source, target) in enumerate(
-            ((start_ref, fields_ref), (end_ref, later_ref))
-        ):
-            pltpu.make_async_copy(
-                source.at[field, :, window, :], target.at[field], local_sems.at[number]
-            ).start()
-    load_weights = pltpu.make_async_copy(
-        plane_weight_ref.at[jnp.minimum(lib, 1)], weights_ref, local_sems.at[2]
+    load(start_ref, fields_ref, edge_lib, 0)
+    load_edge_weights = pltpu.make_async_copy(
+        plane_weight_ref.at[jnp.minimum(edge_lib, 1), :, 1], weights_ref.at[:, 1], local_sems.at[2]
+    )
+    load_own_weights = pltpu.make_async_copy(
+        plane_weight_ref.at[jnp.minimum(lib, 1), :, 0], weights_ref.at[:, 0], local_sems.at[8]
     )
     load_depth = pltpu.make_async_copy(depth_weight_ref, depth_ref, local_sems.at[3])
     load_keys = pltpu.make_async_copy(keys_hbm_ref, keys_ref, local_sems.at[5])
@@ -422,22 +436,22 @@
 
     near = [chips.device(d) for d in (1, 2, 3, 4, 8, 12, 16, 32, 48)]
     near += [{"sub": sub, "lib": (lib + step) % 4} for step in (1, 2, 3)]
-    for device in near:
-        pl.semaphore_signal(barrier, inc=1, device_id=device, device_id_type=MESH)
     sends = sub < 31
     receives = sub > 0
-
-    @pl.when(sends)
-    def _():
-        pl.semaphore_signal(barrier, inc=1, device_id=next_sub, device_id_type=MESH)
 
     @pl.when(receives)
     def _():
         pl.semaphore_signal(barrier, inc=1, device_id=last_sub, device_id_type=MESH)
 
-    load_weights.start()
+    for device in near:
+        pl.semaphore_signal(barrier, inc=1, device_id=device, device_id_type=MESH)
+    load(end_ref, later_ref, edge_lib, 1)
+    load_edge_weights.start()
     load_depth.start()
     load_keys.start()
+    load(start_ref, own_fields_ref, lib, 6)
+    load(end_ref, own_later_ref, lib, 7)
+    load_own_weights.start()
     load_exponents.wait()
     code = jnp.zeros((1, 128), f32)
     for place in range(7):
@@ -446,10 +460,13 @@
     lane = lax.broadcasted_iota(jnp.int32, (8, 128), 1)
     codes_ref[4] = jnp.where(lane < 4, TARGET_CODE + lane, -1).astype(f32)
 
-    pltpu.make_async_copy(fields_ref, fields_ref, local_sems.at[0]).wait()
-    pltpu.make_async_copy(later_ref, later_ref, local_sems.at[1]).wait()
-    products(fields_ref, later_ref, wide_ref, theta_ref, rest_ref)
-    pl.semaphore_wait(barrier, len(near) + jnp.minimum(sub, 1) + jnp.minimum(31 - sub, 1))
+    loaded(fields_ref, 0)
+    widen(fields_ref, wide_ref, 0)
+    products(wide_ref, theta_ref, rest_ref, False)
+    loaded(later_ref, 1)
+    widen(later_ref, wide_ref, 4)
+    products(wide_ref, theta_ref, rest_ref, True)
+    pl.semaphore_wait(barrier, len(near) + jnp.minimum(31 - sub, 1))
     for device in near[6:9]:
         pl.semaphore_signal(ready_sems.at[0], inc=1, device_id=device, device_id_type=MESH)
     code_copies = [
@@ -465,7 +482,7 @@
     ]
     for copy in code_copies:
         copy.start()
-    load_weights.wait()
+    load_edge_weights.wait()
     plane_sums(weights_ref, theta_ref, rest_ref, rest_sum_ref, plane_ref, 1)
     pl.semaphore_wait(ready_sems.at[0], 3)
     for device in near[3:6]:
@@ -501,6 +518,13 @@
         copy.wait()
         part = (lib + 3 - step) % 4
         send_edge(2 + step, codes_ref[part, :1, :], pl.multiple_of(part * 128, 128), 128)
+    loaded(own_fields_ref, 6)
+    widen(own_fields_ref, wide_ref, 0)
+    products(wide_ref, theta_ref, rest_ref, False)
+    loaded(own_later_ref, 7)
+    widen(own_later_ref, wide_ref, 4)
+    products(wide_ref, theta_ref, rest_ref, True)
+    load_own_weights.wait()
     plane_sums(weights_ref, theta_ref, rest_ref, rest_sum_ref, plane_ref, 0)
     depth_sums(plane_ref, depth_ref, table_ref, True)
     both = jnp.dot(pick_ref[...], table_ref[...], preferred_element_type=f32)
@@ -629,11 +653,6 @@
     )
 
 
-def split_result(result_ref, coef_ref, fit_ref):
-    coef_ref[...] = result_ref[:4]
-    fit_ref[...] = result_ref[8:12]
-
-
 def local(snap_start, snap_end, exponents):
     vmem = pl.BlockSpec(memory_space=pltpu.VMEM)
     anywhere = pl.BlockSpec(memory_space=pl.ANY)
@@ -645,6 +664,8 @@
         scratch_shapes=[
             pltpu.VMEM((7, 128), jnp.int32),
             pltpu.VMEM((1, KEYS), f32),
+            pltpu.VMEM((4, CELLS_X, CELLS_Y, WIDTH_Z), bf16),
+            pltpu.VMEM((4, CELLS_X, CELLS_Y, WIDTH_Z), bf16),
             pltpu.VMEM((4, CELLS_X, CELLS_Y, WIDTH_Z), bf16),
             pltpu.VMEM((4, CELLS_X, CELLS_Y, WIDTH_Z), bf16),
             pltpu.VMEM((2, 2, 2 * CENTERS_Y * PAD, MAIN), bf16),
@@ -667,7 +688,7 @@
             pltpu.VMEM((2, CHIPS, CHUNK, 128), f32),
             pltpu.VMEM((TERMS, 2 * TERMS), bf16),
             pltpu.VMEM((8, TERMS), f32),
-            pltpu.SemaphoreType.DMA((6,)),
+            pltpu.SemaphoreType.DMA((9,)),
             pltpu.SemaphoreType.DMA((6,)),
             pltpu.SemaphoreType.DMA((10,)),
             pltpu.SemaphoreType.DMA((4,)),
@@ -688,16 +709,7 @@
         jnp.asarray(plane_weights()),
         jnp.asarray(depth_weights()),
     )
-    return pl.pallas_call(
-        split_result,
-        out_shape=(
-            jax.ShapeDtypeStruct((4, TERMS // 4), f32),
-            jax.ShapeDtypeStruct((4, TESTS), f32),
-        ),
-        in_specs=[vmem],
-        out_specs=(vmem, vmem),
-        name="split_result",
-    )(result)
+    return result[:4], result[8:12]
 
 
 def solution(mesh):

time: 43.7 us -> 43.4 us (level)
  Pallas kernels: 42.9 us -> 41.3 us
  local copies, waits for them, and re-layouts: 0 us -> 1.26 us
    pallas_call x1 -> x0, Pallas kernels: 1.28 us -> none  [local(): pl.pallas_call(split_result, out_shape=(jax.ShapeDtypeStruct((4, TERMS //...]
    slice x0 -> x1, local copies, waits for them, and re-layouts: none -> 1.26 us  [local(): return (result[:4], result[8:12])]
where the time goes in v7:
time: 43.4 us; the launch traced here: 43.2 us
  Pallas kernels  41.3 us (95%)
  local copies, waits for them, and re-layouts  1.26 us (3%)
  between operations  0.64 us (1%)
    pallas_call x1, Pallas kernels, local(): pl.pallas_call(kernel, out_shape=jax.ShapeDtypeStruct((16, TESTS), f32),...  41.3 us
    slice x1, local copies, waits for them, and re-layouts, local(): return (result[:4], result[8:12])  1.26 us

profile of v7, /device:TPU:1, one launch (start us, length us, event | category | flops | bytes accessed | tf_op | source)
XLA Modules:
  0.0 43.2 jit_solution(10546891694403976206)
XLA Ops:
  0.6 41.3 %weak_form_fit.1 = f32[16,128]{1,0:T(8,128)} custom-call(s32[7,128]{1,0:T(8,128)} %bitcast.1, f32[1,1632]{1,0:T(1,128)} %constant.6.clone.keys_hbm_ref, bf16[4,8,128,256]{3,2,1,0:T(8,128)(2,1)} %start_ref.1, bf16[4,8,128,256]{3,2,1,0:T(8,128)(2,1)} %end_ref.1, bf16[2,2,2,128,256]{4,3,2,1,0:T(8,128)(2,1)} %constant.7.clone.plane_weight_ref, ...), custom_call_target="tpu_custom_call" | custom-call | tf_op jit(solution)/shard_map/weak_form_fit/pallas_call | solution.py:659
  42.0 1.3 %fusion = (f32[4,128]{1,0:T(4,128)}, f32[4,128]{1,0:T(4,128)}) fusion(f32[16,128]{1,0:T(8,128)} %weak_form_fit.1), kind=kLoop, calls=%fused_computation | loop fusion | bytes 8192 | tf_op jit(solution)/shard_map/slice | solution.py:712

commit v8 on v7

--- a/solution.py
+++ b/solution.py
@@ -313,8 +313,9 @@
         high = rows.astype(bf16)
         low = (rows - high.astype(f32)).astype(bf16)
         stacked = jnp.concatenate([high, low], axis=0)
-        both = jnp.dot(stacked, normal_ref[...], preferred_element_type=f32)
-        return both[:8, :TERMS] + both[:8, TERMS:] + both[8:, :TERMS]
+        first = jnp.dot(stacked, normal_ref[:, :TERMS], preferred_element_type=f32)
+        second = jnp.dot(high, normal_ref[:, TERMS:], preferred_element_type=f32)
+        return first[:8] + first[8:] + second
 
     def fold(column):
         sums = [jnp.zeros((8, TERMS), f32) for _ in range(4)]
@@ -515,7 +516,7 @@
     send_edge(0, code, pl.multiple_of(lib * 128, 128), 128)
     send_edge(1, codes_ref[4, :1, :], TERMS, 16)
     for step, copy in enumerate(code_copies):
-        copy.wait()
+        copy.wait_recv()
         part = (lib + 3 - step) % 4
         send_edge(2 + step, codes_ref[part, :1, :], pl.multiple_of(part * 128, 128), 128)
     loaded(own_fields_ref, 6)
@@ -529,11 +530,6 @@
     depth_sums(plane_ref, depth_ref, table_ref, True)
     both = jnp.dot(pick_ref[...], table_ref[...], preferred_element_type=f32)
     lib_ref[...] = both[:, :TESTS] + both[:, TESTS:]
-    @pl.when(sends)
-    def _():
-        for edge in edges:
-            edge.wait_send()
-
     @pl.when(receives)
     def _():
         for edge in edges:
@@ -583,7 +579,7 @@
         pair.start()
         pairs.append(pair)
     for pair in pairs:
-        pair.wait()
+        pair.wait_recv()
     half_in_ref[...] = half_in_ref[...] + half_ref[core]
     pl.semaphore_wait(ready_sems.at[1], 3)
     own = chips.chip(0)
@@ -609,9 +605,7 @@
             device_id=chips.device(d),
             device_id_type=MESH,
         ).start()
-    pltpu.make_async_copy(received, received, part_sems.at[0]).wait()
     pltpu.make_async_copy(received, received, done_sems.at[1]).wait()
-    pltpu.make_async_copy(received, received, done_sems.at[0]).wait()
     swap = pltpu.make_async_remote_copy(
         src_ref=done_ref.at[core],
         dst_ref=done_ref.at[core],
@@ -621,7 +615,7 @@
         device_id_type=MESH,
     )
     swap.start()
-    swap.wait()
+    swap.wait_recv()
     for half in range(2):
         for number, (i, j) in enumerate(BLOCKS[half][:4]):
             lanes = slice(j * 128, j * 128 + 128)
@@ -651,6 +645,18 @@
     solve(
         gram_ref, normal_ref, lib_ref, cross_sum, square_sum, lib, result_ref, spot_ref
     )
+    for copy in code_copies:
+        copy.wait_send()
+    for pair in pairs:
+        pair.wait_send()
+    pltpu.make_async_copy(received, received, part_sems.at[0]).wait()
+    pltpu.make_async_copy(received, received, done_sems.at[0]).wait()
+    swap.wait_send()
+
+    @pl.when(sends)
+    def _():
+        for edge in edges:
+            edge.wait_send()
 
 
 def local(snap_start, snap_end, exponents):

time: 43.4 us -> 43 us (level)
  no operation moved by 1% of the time
where the time goes in v8:
time: 43 us; the launch traced here: 42.8 us
  Pallas kernels  40.9 us (95%)
  local copies, waits for them, and re-layouts  1.26 us (3%)
  between operations  0.64 us (1%)
    pallas_call x1, Pallas kernels, local(): pl.pallas_call(kernel, out_shape=jax.ShapeDtypeStruct((16, TESTS), f32),...  40.9 us
    slice x1, local copies, waits for them, and re-layouts, local(): return (result[:4], result[8:12])  1.26 us

profile of v8, /device:TPU:1, one launch (start us, length us, event | category | flops | bytes accessed | tf_op | source)
XLA Modules:
  0.0 42.8 jit_solution(8546015552956200769)
XLA Ops:
  0.6 40.9 %weak_form_fit.1 = f32[16,128]{1,0:T(8,128)} custom-call(s32[7,128]{1,0:T(8,128)} %bitcast.1, f32[1,1632]{1,0:T(1,128)} %constant.6.clone.keys_hbm_ref, bf16[4,8,128,256]{3,2,1,0:T(8,128)(2,1)} %start_ref.1, bf16[4,8,128,256]{3,2,1,0:T(8,128)(2,1)} %end_ref.1, bf16[2,2,2,128,256]{4,3,2,1,0:T(8,128)(2,1)} %constant.7.clone.plane_weight_ref, ...), custom_call_target="tpu_custom_call" | custom-call | tf_op jit(solution)/shard_map/weak_form_fit/pallas_call | solution.py:665
  41.6 1.3 %fusion = (f32[4,128]{1,0:T(4,128)}, f32[4,128]{1,0:T(4,128)}) fusion(f32[16,128]{1,0:T(8,128)} %weak_form_fit.1), kind=kLoop, calls=%fused_computation | loop fusion | bytes 8192 | tf_op jit(solution)/shard_map/slice | solution.py:718

commit v9 on v8

--- a/solution.py
+++ b/solution.py
@@ -205,8 +205,8 @@
             some(MAIN + at, lanes, put)
         return carry
 
-    lax.fori_loop(0, MAIN // 16, main_rows, 0)
-    lax.fori_loop(0, REST // 16, rest_rows, 0)
+    lax.fori_loop(0, MAIN // 16, main_rows, 0, unroll=4 if changes else 2)
+    lax.fori_loop(0, REST // 16, rest_rows, 0, unroll=4 if changes else 2)
     used = PRODUCTS % 4 * REST
     rest_ref[PRODUCTS // 4, used:, :] = jnp.zeros((4 * REST - used, WIDTH_Z), bf16)
 
@@ -578,9 +578,10 @@
         )
         pair.start()
         pairs.append(pair)
-    for pair in pairs:
+    for group, pair in enumerate(pairs):
         pair.wait_recv()
-    half_in_ref[...] = half_in_ref[...] + half_ref[core]
+        chunks = pl.ds(group * CHIPS // 2, CHIPS // 2)
+        half_in_ref[chunks] = half_in_ref[chunks] + half_ref[core, chunks]
     pl.semaphore_wait(ready_sems.at[1], 3)
     own = chips.chip(0)
     for d in PARTNERS:

time: 43 us -> 42.9 us (level)
  no operation moved by 1% of the time
where the time goes in v9:
time: 42.9 us; the launch traced here: 42.7 us
  Pallas kernels  40.8 us (95%)
  local copies, waits for them, and re-layouts  1.26 us (3%)
  between operations  0.64 us (1%)
    pallas_call x1, Pallas kernels, local(): pl.pallas_call(kernel, out_shape=jax.ShapeDtypeStruct((16, TESTS), f32),...  40.8 us
    slice x1, local copies, waits for them, and re-layouts, local(): return (result[:4], result[8:12])  1.26 us

profile of v9, /device:TPU:1, one launch (start us, length us, event | category | flops | bytes accessed | tf_op | source)
XLA Modules:
  0.0 42.7 jit_solution(6184464396888216521)
XLA Ops:
  0.6 40.8 %weak_form_fit.1 = f32[16,128]{1,0:T(8,128)} custom-call(s32[7,128]{1,0:T(8,128)} %bitcast.1, f32[1,1632]{1,0:T(1,128)} %constant.6.clone.keys_hbm_ref, bf16[4,8,128,256]{3,2,1,0:T(8,128)(2,1)} %start_ref.1, bf16[4,8,128,256]{3,2,1,0:T(8,128)(2,1)} %end_ref.1, bf16[2,2,2,128,256]{4,3,2,1,0:T(8,128)(2,1)} %constant.7.clone.plane_weight_ref, ...), custom_call_target="tpu_custom_call" | custom-call | tf_op jit(solution)/shard_map/weak_form_fit/pallas_call | solution.py:666
  41.5 1.3 %fusion = (f32[4,128]{1,0:T(4,128)}, f32[4,128]{1,0:T(4,128)}) fusion(f32[16,128]{1,0:T(8,128)} %weak_form_fit.1), kind=kLoop, calls=%fused_computation | loop fusion | bytes 8192 | tf_op jit(solution)/shard_map/slice | solution.py:719
